TPU v7x, 256 devices: a whole 4x4x8 slice. The times are simulated.
256 devices in a mesh: dp: 32 (over z_lo, x, y), hid: 8 (over z_hi, core).
Axes of the slice: x: 4, y: 4, z: 8 (z_hi: 4, z_lo: 2; z = z_hi * 2 + z_lo), core: 2. Of those that a mesh axis runs over, the one named last changes fastest.
Arguments:
- tokens: bfloat16 [4096, 4096], P('dp', 'hid'), may hold values from -6 to 6
- cotangent: bfloat16 [4096, 4096], P('dp', 'hid'), may hold values from -6 to 6
- routes: int32 [4096, 2], P('dp'), may hold values from 0 to 63, as said below
- gates: float32 [4096, 2], P('dp'), may hold values from 0.2 to 1
- fetch: int32 [32, 2], replicated, may hold values from 0 to 63, as said below
- w_in: bfloat16 [64, 2, 1024, 4096], P('dp', None, 'hid'), may hold values from -0.09375 to 0.09375
- w_down: bfloat16 [64, 1024, 4096], P('dp', 'hid'), may hold values from -0.1875 to 0.1875
Outputs:
- outputs: bfloat16 [4096, 4096], P('dp', 'hid')
- token_grads: bfloat16 [4096, 4096], P('dp', 'hid')
- grad_in: bfloat16 [64, 2, 1024, 4096], P('dp', None, 'hid')
- grad_down: bfloat16 [64, 1024, 4096], P('dp', 'hid')
Inputs may be any that keep to these rules, and one draw needn't show every extreme that they name: fetch[r, 0] is an expert owned by dp index r - 1 and fetch[r, 1] one owned by index r + half the dp axis, cyclically; expert e is owned by index e // 2. `routes`: the 2 ids of a token are different candidates of its own dp index (its 2 experts and its two fetched ones); among the tokens of one index no candidate is named more than 96 times, and one is named exactly 96 times.
All inputs are finite; a program needn't handle non-finite values.
Results may differ from a plain program's by a relative error of at most 0.0061.
Values may be sent and summed in bfloat16 or wider, within the bound.
No kernel may reach another device: no remote copies, remote signals or barrier semaphores. Data moves between devices by JAX's collectives and lax.ppermute only.
A program may use at most 128 MiB of HBM per device.

v0:
```python
import jax
import jax.numpy as jnp
from jax import lax
from jax.experimental import pallas as pl
from jax.experimental.pallas import tpu as pltpu
from jax.sharding import Mesh
from jax.sharding import PartitionSpec as P

AXES = ("zlo", "x", "y", "zhi", "core")
DP = ("zlo", "x", "y")
HID = ("zhi", "core")
RING = 8
SLICE = 512
NT = (((1,), (1,)), ((), ()))
MIB = 1024 * 1024
BF = jnp.bfloat16


def ring_index(z):
    return (z % 2) * 4 + z // 2


def along_z(array, by):
    pairs = [(ring_index(z), ring_index((z + by) % RING)) for z in range(RING)]
    return lax.ppermute(array, ("zlo", "zhi"), pairs)


def along_plane(array, by):
    return lax.ppermute(array, ("x", "y"), [(i, (i + by) % 16) for i in range(16)])


def along_dp(array, by):
    return lax.ppermute(array, DP, [(i, (i + by) % 32) for i in range(32)])


def other_core(array):
    return lax.ppermute(array, "core", [(0, 1), (1, 0)])


def together(*arrays):
    return lax.optimization_barrier(arrays)


def wide(a):
    return a.astype(jnp.float32)


def narrow(a):
    return a.astype(BF)


def dot(a, b, dims=None):
    if dims is None:
        return jnp.dot(a, b, preferred_element_type=jnp.float32)
    return lax.dot_general(a, b, dims, preferred_element_type=jnp.float32)


def columns(slot):
    return pl.ds(pl.multiple_of(slot * SLICE, SLICE), SLICE)


def rows_of(expert, height):
    return pl.ds(pl.multiple_of(expert * height, height), height)


def core_of(where, i):
    return jnp.where(i < 4, where[3], 1 - where[3])


def near_slot(where, i):
    return ((where[2] + 2 * (i % 4) + 6) % RING) // 2 * 2 + core_of(where, i)


def far_slot(where, i):
    return ((where[2] + 2 * (i % 4) + 5) % RING) // 2 * 2 + core_of(where, i)


def left_slot(where, i):
    return jnp.where(where[4] == 1, far_slot(where, i), near_slot(where, i))


def far_place(where, i):
    quarter = near_slot(where, i) // 2
    low = where[2] % 2
    return ((2 * quarter + 1 - low - where[2] + 3 + RING) % RING) // 2 + i // 4 * 4


def turned(a):
    return narrow(wide(a).T)


def gradients(weight, pre, back, turn, base):
    gate_pre, up_proj = pre[:, :128], pre[:, 128:]
    back_hid = weight * back
    sig = 1.0 / (1.0 + jnp.exp(-gate_pre))
    active = gate_pre * sig
    slope = sig * (1.0 + gate_pre * (1.0 - sig))
    hidden = narrow(weight * (active * up_proj))
    grads = narrow(back_hid * up_proj * slope), narrow(back_hid * active)
    for h, value in enumerate((*grads, hidden)):
        turn[base, 128 * h : 128 * h + 128, :] = turned(value)
    return hidden, grads


def weight_loads(sources, bufs, sems, slot, rows):
    return [
        pltpu.make_async_copy(source.at[row, columns(slot)], buf.at[slot], sem.at[slot])
        for source, buf, sem, row in zip(sources, bufs, sems, rows)
    ]


def chunk_loads(refs, buf, sem):
    return [pltpu.make_async_copy(refs[i], buf.at[i], sem.at[i]) for i in range(8)]


def left_loads(refs, buf, sem):
    copies = []
    for part, base in ((0, 0), (2, 4)):
        for ref, places in zip(refs[part : part + 2], ((1, 2), (0, 3))):
            for h, place in enumerate(places):
                at = base + place
                copies.append(pltpu.make_async_copy(ref.at[h], buf.at[at], sem.at[at]))
    return copies


def projections(buf, slots, w_in, w_down):
    pre = None
    back = None
    for i, slot in enumerate(slots):
        p = dot(buf[i, 0], w_in(slot), NT)
        b = dot(buf[i, 1], w_down(slot), NT)
        pre = p if pre is None else pre + p
        back = b if back is None else back + b
    return pre, back


def row_parts(out, peer, slots, hidden, grads, w_in, w_down):
    for i in (7, 6, 5, 4, 3, 2, 1, 0):
        ref = out if i < 4 else peer
        ref[i % 4, 0] = narrow(dot(hidden, w_down(slots[i])))
        ref[i % 4, 1] = narrow(dot(grads, w_in(slots[i])))


def near_kernel(where, weights, w_in, w_down, *refs):
    own, far = refs[:8], refs[8:16]
    own_out, own_peer, far_out, far_peer, turn = refs[16:21]
    xo, xf, wbuf, dbuf, so, sf, sw, sd = refs[21:]
    own_slots = [near_slot(where, i) for i in range(8)]
    far_slots = [far_slot(where, i) for i in range(8)]
    rows = pl.ds(0, 512), pl.ds(0, 256)
    own_copies = chunk_loads(own, xo, so)
    far_copies = chunk_loads(far, xf, sf)
    matrices = [
        weight_loads((w_in, w_down), (wbuf, dbuf), (sw, sd), slot, rows) for slot in own_slots
    ]
    for copy, pair in zip(own_copies, matrices):
        copy.start()
        for load in pair:
            load.start()
    for copy in far_copies:
        copy.start()
    pre = None
    back = None
    for i, slot in enumerate(own_slots):
        own_copies[i].wait()
        for load in matrices[i]:
            load.wait()
        p = dot(xo[i, 0], wbuf[slot], NT)
        b = dot(xo[i, 1], dbuf[slot], NT)
        pre = p if pre is None else pre + p
        back = b if back is None else back + b
    for copy in far_copies:
        copy.wait()
    first = gradients(weights[:, 0:1], pre[:, :256], back[:, :128], turn, 0)
    second = gradients(weights[:, 1:2], pre[:, 256:], back[:, 128:], turn, 1)
    far_in, far_down = rows_of(where[1], 256), rows_of(where[1], 128)

    def far_w(slot):
        return wbuf[slot, far_in, :]

    def far_d(slot):
        return dbuf[slot, far_down, :]

    pre, back = projections(xf, far_slots, far_w, far_d)
    third = gradients(weights[:, 3:4], pre, back, turn, 2)
    row_parts(
        own_out,
        own_peer,
        own_slots,
        jnp.concatenate([first[0], second[0]], axis=1),
        jnp.concatenate([*first[1], *second[1]], axis=1),
        lambda slot: wbuf[slot],
        lambda slot: dbuf[slot],
    )
    row_parts(
        far_out,
        far_peer,
        far_slots,
        third[0],
        jnp.concatenate(third[1], axis=1),
        far_w,
        far_d,
    )


def left_kernel(where, weights, w_in, w_down, *refs):
    left, (out, peer, turn) = refs[:4], refs[4:7]
    xl, wbuf, dbuf, sl, sw, sd = refs[7:]
    slots = [left_slot(where, i) for i in range(8)]
    rows = rows_of(where[0], 256), rows_of(where[0], 128)
    copies = left_loads(left, xl, sl)
    matrices = [
        weight_loads((w_in, w_down), (wbuf, dbuf), (sw, sd), slot, rows) for slot in slots
    ]
    for copy, pair in zip(copies, matrices):
        copy.start()
        for load in pair:
            load.start()
    for copy in copies:
        copy.wait()
    pre = None
    back = None
    for i, slot in enumerate(slots):
        for load in matrices[i]:
            load.wait()
        p = dot(xl[i, 0], wbuf[slot], NT)
        b = dot(xl[i, 1], dbuf[slot], NT)
        pre = p if pre is None else pre + p
        back = b if back is None else back + b
    hidden, grads = gradients(weights[:, 2:3], pre, back, turn, 0)
    row_parts(
        out,
        peer,
        slots,
        hidden,
        jnp.concatenate(grads, axis=1),
        lambda slot: wbuf[slot],
        lambda slot: dbuf[slot],
    )


def weights_kernel(where, turn, left_turn, *refs):
    own, left, far = refs[:8], refs[8:12], refs[12:20]
    din, ddown = refs[20:22]
    xo, xl, xf, sum_in, sum_down, bin_, bdown, so, sl, sf, si, sd = refs[22:]
    copies = chunk_loads(own, xo, so) + left_loads(left, xl, sl) + chunk_loads(far, xf, sf)
    for copy in copies:
        copy.start()
    for copy in copies:
        copy.wait()
    left_in, left_down = rows_of(where[0], 256), rows_of(where[0], 128)
    far_in, far_down = rows_of(where[1], 256), rows_of(where[1], 128)

    def stores(i):
        cols = columns(near_slot(where, i))
        return (
            pltpu.make_async_copy(bin_.at[i], din.at[:, cols], si.at[i]),
            pltpu.make_async_copy(bdown.at[i], ddown.at[:, cols], sd.at[i]),
        )

    def step(i, carry):
        far_at = far_place(where, i)
        left_at = jnp.where(where[4] == 1, far_at, i)
        for e in range(2):
            sum_in[256 * e : 256 * e + 256, :] = dot(turn[e, :256, :], xo[i, 0])
            sum_down[128 * e : 128 * e + 128, :] = dot(turn[e, 256:, :], xo[i, 1])
        sum_in[left_in, :] += dot(left_turn[0, :256, :], xl[left_at, 0])
        sum_down[left_down, :] += dot(left_turn[0, 256:, :], xl[left_at, 1])
        sum_in[far_in, :] += dot(turn[2, :256, :], xf[far_at, 0])
        sum_down[far_down, :] += dot(turn[2, 256:, :], xf[far_at, 1])
        bin_[i] = narrow(sum_in[...])
        bdown[i] = narrow(sum_down[...])
        for copy in stores(i):
            copy.start()
        return carry

    def finish(i, carry):
        for copy in stores(i):
            copy.wait()
        return carry

    lax.fori_loop(0, 8, step, 0)
    lax.fori_loop(0, 8, finish, 0)


SMEM = pl.BlockSpec(memory_space=pltpu.SMEM)
VMEM = pl.BlockSpec(memory_space=pltpu.VMEM)
FAR_MEMORY = pl.BlockSpec(memory_space=pltpu.HBM)
DMA = pltpu.SemaphoreType.DMA


def shape(*dims, dtype=BF):
    return jax.ShapeDtypeStruct(dims, dtype)


def in_hbm(a):
    return pltpu.with_memory_space_constraint(a, pltpu.HBM)


def params(mib):
    return pltpu.CompilerParams(vmem_limit_bytes=mib * MIB)


QUAD = shape(4, 2, 128, SLICE)
CHUNKS = pltpu.VMEM((8, 2, 128, SLICE), BF)


def shards(tokens, cotangent, routes, gates, fetch, w_in, w_down):
    my_row = lax.axis_index(DP)
    z = lax.axis_index("zhi") * 2 + lax.axis_index("zlo")
    core = lax.axis_index("core")
    plane = my_row % 16
    first, last = plane == 0, plane == 15
    both = jnp.stack([tokens, cotangent])

    candidates = jnp.concatenate(
        [my_row * 2 + jnp.arange(2, dtype=jnp.int32), fetch[my_row]]
    )
    matches = routes[:, :, None] == candidates[None, None, :]
    combine = jnp.sum(jnp.where(matches, gates[:, :, None], 0.0), axis=1)
    need_left = fetch[(my_row + 1) % 32, 0] - my_row * 2
    need_far = fetch[(my_row + 16) % 32, 1] - my_row * 2
    where = jnp.stack([need_left, need_far, z, core, last.astype(jnp.int32)]).astype(jnp.int32)

    def leftward(pairs):
        chosen = [jnp.where(first, got[k - 1], got[k]) for k in pairs]
        return along_plane(jnp.stack(chosen), -1)

    got = {0: both}
    got[-1], got[1] = along_z(both, 1), along_z(both, -1)
    from_far = along_dp(combine[:, 2:4], 16)
    got[-1], got[1], from_far, where = together(got[-1], got[1], from_far, where)
    got[-2], got[2] = along_z(got[-1], 1), along_z(got[1], -1)
    from_left = along_plane(jnp.where(first, from_far[:, 0:1], combine[:, 2:3]), -1)
    got[-2], got[2], from_left = together(got[-2], got[2], from_left)
    weights = jnp.concatenate([combine[:, :2], from_left, from_far[:, 1:2]], axis=1)
    got[-3], got[3] = along_z(got[-2], 1), along_z(got[2], -1)
    early = leftward((0, 2))
    got[-3], got[3], weights = together(got[-3], got[3], weights)
    up, down = along_z(got[-3][0], 1), along_z(got[3][1], -1)
    up, down, early = together(up, down, early)
    got[4] = jnp.stack([up, down])
    own = [got[k] for k in (-2, 0, 2, 4)]
    far = [got[k] for k in (-3, -1, 1, 3)]
    own_peers = [other_core(a) for a in own]
    far_peers = [other_core(a) for a in far]
    got[4], *own_peers = together(got[4], *own_peers)
    own = own[:3] + [got[4]] + [in_hbm(a) for a in own_peers]
    far = far + [in_hbm(a) for a in far_peers]
    late = leftward((-2, 4))

    flat_in = in_hbm(w_in.reshape(512, 4096))
    flat_down = in_hbm(w_down.reshape(256, 4096))
    own_out, own_peer, far_out, far_peer, turn = pl.pallas_call(
        near_kernel,
        out_shape=(QUAD,) * 4 + (shape(3, 384, 128),),
        in_specs=[SMEM, VMEM] + [FAR_MEMORY] * 18,
        out_specs=(VMEM,) * 5,
        scratch_shapes=[
            CHUNKS,
            CHUNKS,
            pltpu.VMEM((8, 512, SLICE), BF),
            pltpu.VMEM((8, 256, SLICE), BF),
            DMA((8,)),
            DMA((8,)),
            DMA((8,)),
            DMA((8,)),
        ],
        compiler_params=params(16),
        name="near",
    )(where, weights, flat_in, flat_down, *own, *far)
    late, turn = together(late, turn)
    lefts = [early, late, other_core(early), other_core(late)]
    left_out, left_peer, left_turn = pl.pallas_call(
        left_kernel,
        out_shape=(QUAD,) * 2 + (shape(1, 384, 128),),
        in_specs=[SMEM, VMEM] + [FAR_MEMORY] * 6,
        out_specs=(VMEM,) * 3,
        scratch_shapes=[
            CHUNKS,
            pltpu.VMEM((8, 256, SLICE), BF),
            pltpu.VMEM((8, 128, SLICE), BF),
            DMA((8,)),
            DMA((8,)),
            DMA((8,)),
        ],
        compiler_params=params(10),
        name="left",
    )(where, weights, flat_in, flat_down, *lefts)
    own_peer, far_peer = other_core(own_peer), other_core(far_peer)
    left_peer = other_core(left_peer)

    def rightward(i):
        return along_plane(narrow(wide(left_out[i]) + wide(left_peer[i])), 1)

    right = {3: rightward(3)}
    grad_in, grad_down = pl.pallas_call(
        weights_kernel,
        out_shape=(shape(512, 4096), shape(256, 4096)),
        in_specs=[SMEM, VMEM, VMEM] + [FAR_MEMORY] * 20,
        out_specs=(FAR_MEMORY, FAR_MEMORY),
        scratch_shapes=[
            CHUNKS,
            CHUNKS,
            CHUNKS,
            pltpu.VMEM((512, SLICE), jnp.float32),
            pltpu.VMEM((256, SLICE), jnp.float32),
            pltpu.VMEM((8, 512, SLICE), BF),
            pltpu.VMEM((8, 256, SLICE), BF),
            DMA((8,)),
            DMA((8,)),
            DMA((8,)),
            DMA((8,)),
            DMA((8,)),
        ],
        compiler_params=params(16),
        name="weights",
    )(where, turn, left_turn, *own, *lefts, *far)
    right[3], grad_in, grad_down = together(right[3], grad_in, grad_down)

    def near_part(i, half=slice(None)):
        extra = jnp.where(first, 0.0, wide(right[i][half]))
        return wide(own_out[i][half]) + wide(own_peer[i][half]) + extra

    def far_part(i):
        extra = jnp.where(first, wide(right[i]), 0.0)
        return wide(far_out[i]) + wide(far_peer[i]) + extra

    top = narrow(near_part(3))
    up, down = along_z(top[0], 1), along_z(top[1], -1)
    right[0] = rightward(0)
    up, down, right[0] = together(up, down, right[0])
    high, low = far_part(3), far_part(0)
    up = narrow(jnp.stack([high[0] + wide(up), high[1]]))
    down = narrow(jnp.stack([low[0], low[1] + wide(down)]))
    up, down = along_z(up, 1), along_z(down, -1)
    right[2] = rightward(2)
    up, down, right[2] = together(up, down, right[2])
    up, down = narrow(near_part(2) + wide(up)), narrow(near_part(0) + wide(down))
    up, down = along_z(up, 1), along_z(down, -1)
    right[1] = rightward(1)
    up, down, right[1] = together(up, down, right[1])
    up, down = narrow(far_part(2) + wide(up)), narrow(far_part(1) + wide(down))
    up, down = along_z(up, 1), along_z(down, -1)
    total = narrow(near_part(1) + wide(up) + wide(down))
    return total[0], total[1], grad_in.reshape(w_in.shape), grad_down.reshape(w_down.shape)


def solution(mesh):
    fine = Mesh(mesh.devices.reshape(2, 4, 4, 4, 2), AXES)
    return jax.shard_map(
        shards,
        mesh=fine,
        in_specs=(
            P(DP, HID),
            P(DP, HID),
            P(DP, None),
            P(DP, None),
            P(),
            P(DP, None, HID, None),
            P(DP, HID, None),
        ),
        out_specs=(
            P(DP, HID),
            P(DP, HID),
            P(DP, None, HID, None),
            P(DP, HID, None),
        ),
        check_vma=False,
    )
```

profile of v0, /device:TPU:0, one launch (start us, length us, event | category | flops | bytes accessed | tf_op | source)
XLA Modules:
  0.0 119.7 jit_solution(16510952225360106701)
XLA Ops:
  1.9 4.0 %collective-permute-start.1 = (bf16[2,128,512]{2,1,0:T(8,128)(2,1)S(1)}, bf16[2,128,512]{2,1,0:T(8,128)(2,1)S(1)}, u32[]{:S(2)}, u32[]{:S(2)}) collective-permute-start(bf16[2,128,512]{2,1,0:T(8,128)(2,1)S(1)} %pad_maximum_fusion.2.refs_1_), channel_id=1, source_target_pairs={{0,134},{128,0},{2,128},{130,2},{4,130},{132,4},{6,132},{134,6},{1... | collective-permute-start | bytes 786440 | tf_op jit(solution)/shard_map/ppermute | solution.py:25
  12.6 2.8 %collective-permute-start.4 = (bf16[2,128,512]{2,1,0:T(8,128)(2,1)S(1)}, bf16[2,128,512]{2,1,0:T(8,128)(2,1)S(1)}, u32[]{:S(2)}, u32[]{:S(2)}) collective-permute-start(bf16[2,128,512]{2,1,0:T(8,128)(2,1)S(1)} %collective-permute-done.1.refs_10_.refs_14_), channel_id=1, source_target_pairs={{0,134},{128,0},{2,128},{130,2},{4,130},{132,4},{6,132},{134,6},{1... | collective-permute-start | bytes 786440 | tf_op jit(solution)/shard_map/ppermute | solution.py:25
  15.4 5.2 %collective-permute-start.5 = (f32[128,1]{0,1:T(1,128)S(1)}, f32[128,1]{0,1:T(1,128)S(1)}, u32[]{:S(2)}, u32[]{:S(2)}) collective-permute-start(f32[128,1]{0,1:T(1,128)S(1)} %get-tuple-element.105), channel_id=1, source_target_pairs={{0,120},{8,0},{16,8},{24,16},{32,24},{40,32},{48,40},{56,48},{64,5... | collective-permute-start | bytes 1544 | tf_op jit(solution)/shard_map/ppermute | solution.py:29
  22.7 2.5 %collective-permute-start.7 = (bf16[2,128,512]{2,1,0:T(8,128)(2,1)S(1)}, bf16[2,128,512]{2,1,0:T(8,128)(2,1)S(1)}, u32[]{:S(2)}, u32[]{:S(2)}) collective-permute-start(bf16[2,128,512]{2,1,0:T(8,128)(2,1)S(1)} %collective-permute-done.4.refs_2_), channel_id=1, source_target_pairs={{0,134},{128,0},{2,128},{130,2},{4,130},{132,4},{6,132},{134,6},{1... | collective-permute-start | bytes 786440 | tf_op jit(solution)/shard_map/ppermute | solution.py:25
  25.2 5.6 %collective-permute-start.10 = (bf16[2,2,128,512]{3,2,1,0:T(8,128)(2,1)S(1)}, bf16[2,2,128,512]{3,2,1,0:T(8,128)(2,1)S(1)}, u32[]{:S(2)}, u32[]{:S(2)}) collective-permute-start(bf16[2,2,128,512]{3,2,1,0:T(8,128)(2,1)S(1)} %pad_maximum_fusion), channel_id=1, source_target_pairs={{0,120},{8,0},{16,8},{24,16},{32,24},{40,32},{48,40},{56,48},{64,5... | collective-permute-start | bytes 1572872 | tf_op jit(solution)/shard_map/ppermute | solution.py:29
  31.0 3.3 %collective-permute-start.9 = (bf16[128,512]{1,0:T(8,128)(2,1)S(1)}, bf16[128,512]{1,0:T(8,128)(2,1)S(1)}, u32[]{:S(2)}, u32[]{:S(2)}) collective-permute-start(bf16[128,512]{1,0:T(8,128)(2,1)S(1)} %slice_bitcast_fusion.6), channel_id=1, source_target_pairs={{0,134},{128,0},{2,128},{130,2},{4,130},{132,4},{6,132},{134,6},{1... | collective-permute-start | bytes 393224 | tf_op jit(solution)/shard_map/ppermute | solution.py:25
  34.8 2.3 %collective-permute-done.8 = bf16[128,512]{1,0:T(8,128)(2,1)S(1)} collective-permute-done((bf16[128,512]{1,0:T(8,128)(2,1)S(1)}, bf16[128,512]{1,0:T(8,128)(2,1)S(1)}, u32[]{:S(2)}, u32[]{:S(2)}) %collective-permute-start.8) | collective-permute-done | bytes 131104 | tf_op jit(solution)/shard_map/ppermute | solution.py:25
  37.2 2.1 %collective-permute-done.10.refs_0_.refs_8_ = bf16[2,2,128,512]{3,2,1,0:T(8,128)(2,1)S(1)} collective-permute-done((bf16[2,2,128,512]{3,2,1,0:T(8,128)(2,1)S(1)}, bf16[2,2,128,512]{3,2,1,0:T(8,128)(2,1)S(1)}, u32[]{:S(2)}, u32[]{:S(2)}) %collective-permute-start.10) | collective-permute-done | bytes 524320 | tf_op jit(solution)/shard_map/ppermute | solution.py:29
  41.8 5.8 %collective-permute-start.21 = (bf16[2,2,128,512]{3,2,1,0:T(8,128)(2,1)}, bf16[2,2,128,512]{3,2,1,0:T(8,128)(2,1)S(1)}, u32[]{:S(2)}, u32[]{:S(2)}) collective-permute-start(bf16[2,2,128,512]{3,2,1,0:T(8,128)(2,1)} %pad_maximum_fusion.1), channel_id=1, source_target_pairs={{0,120},{8,0},{16,8},{24,16},{32,24},{40,32},{48,40},{56,48},{64,5... | collective-permute-start | bytes 1572872 | tf_op jit(solution)/shard_map/ppermute | solution.py:29
  50.4 7.9 %near.1 = (bf16[4,2,128,512]{3,2,1,0:T(8,128)(2,1)S(1)}, bf16[4,2,128,512]{3,2,1,0:T(8,128)(2,1)S(1)}, bf16[4,2,128,512]{3,2,1,0:T(8,128)(2,1)S(1)}, bf16[4,2,12...) custom-call(s32[5]{0:T(128)S(1)} %stack.82.where, f32[128,4]{1,0:T(8,128)S(1)} %copy.17.weights, ...), custom_call_target="tpu_custom_call" | custom-call | tf_op jit(solution)/shard_map/near/pallas_call | solution.py:354
  59.4 1.9 %collective-permute-done.23.refs_3_.refs_11_ = bf16[2,2,128,512]{3,2,1,0:T(8,128)(2,1)S(1)} collective-permute-done((bf16[2,2,128,512]{3,2,1,0:T(8,128)(2,1)S(1)}, bf16[2,2,128,512]{3,2,1,0:T(8,128)(2,1)S(1)}, u32[]{:S(2)}, u32[]{:S(2)}) %collective-permute-start.23) | collective-permute-done | bytes 524320 | tf_op jit(solution)/shard_map/ppermute | solution.py:37
  61.3 4.5 %left.1 = (bf16[4,2,128,512]{3,2,1,0:T(8,128)(2,1)S(1)}, bf16[4,2,128,512]{3,2,1,0:T(8,128)(2,1)S(1)}, bf16[1,384,128]{2,1,0:T(8,128)(2,1)S(1)}) custom-call(s32[5]{0:T(128)S(1)} %stack.82.where, f32[128,4]{1,0:T(8,128)S(1)} %copy.17.weights, bf16[512,4096]{1,0:T(8,128)(2,1)} %bitcast.80, bf16[256,4096]{1,0:T(8,128)(2,1)} %bitcast.82, ...), custom_call_target="tpu_custom_call" | custom-call | tf_op jit(solution)/shard_map/left/pallas_call | solution.py:374
  66.5 2.0 %collective-permute-done.24 = bf16[4,2,128,512]{3,2,1,0:T(8,128)(2,1)S(1)} collective-permute-done((bf16[4,2,128,512]{3,2,1,0:T(8,128)(2,1)S(1)}, bf16[4,2,128,512]{3,2,1,0:T(8,128)(2,1)S(1)}, u32[]{:S(2)}, u32[]{:S(2)}) %collective-permute-start.24) | collective-permute-done | bytes 1048608 | tf_op jit(solution)/shard_map/ppermute | solution.py:37
  69.1 8.3 %weights.1 = (bf16[512,4096]{1,0:T(8,128)(2,1)}, bf16[256,4096]{1,0:T(8,128)(2,1)}) custom-call(s32[5]{0:T(128)S(1)} %stack.82.where, bf16[3,384,128]{2,1,0:T(8,128)(2,1)S(1)} %get-tuple-element.72.turn, bf16[1,384,128]{2,1,0:T(8,128)(2,1)S(1)} %get-tuple-element.73.left_turn, bf16[2,128,512]{2,1,0:T(8,128)(2,1)S(1)} %collective-permute-done.3.refs_0_, ...), custom_call_target="tpu_custom_call" | custom-call | tf_op jit(solution)/shard_map/weights/pallas_call | solution.py:397
  77.6 3.9 %collective-permute-done.25 = bf16[2,128,512]{2,1,0:T(8,128)(2,1)S(1)} collective-permute-done((bf16[2,128,512]{2,1,0:T(8,128)(2,1)S(1)}, bf16[2,128,512]{2,1,0:T(8,128)(2,1)S(1)}, u32[]{:S(2)}, u32[]{:S(2)}) %collective-permute-start.25) | collective-permute-done | bytes 262176 | tf_op jit(solution)/shard_map/ppermute | solution.py:29
  81.7 3.2 %collective-permute-start.27 = (bf16[128,512]{1,0:T(8,128)(2,1)S(1)}, bf16[128,512]{1,0:T(8,128)(2,1)S(1)}, u32[]{:S(2)}, u32[]{:S(2)}) collective-permute-start(bf16[128,512]{1,0:T(8,128)(2,1)S(1)} %get-tuple-element.100), channel_id=1, source_target_pairs={{0,134},{128,0},{2,128},{130,2},{4,130},{132,4},{6,132},{134,6},{1... | collective-permute-start | bytes 393224 | tf_op jit(solution)/shard_map/ppermute | solution.py:25
  84.9 5.0 %collective-permute-done.28 = bf16[2,128,512]{2,1,0:T(8,128)(2,1)S(1)} collective-permute-done((bf16[2,128,512]{2,1,0:T(8,128)(2,1)S(1)}, bf16[2,128,512]{2,1,0:T(8,128)(2,1)S(1)}, u32[]{:S(2)}, u32[]{:S(2)}) %collective-permute-start.28) | collective-permute-done | bytes 262176 | tf_op jit(solution)/shard_map/ppermute | solution.py:29
  90.4 3.3 %collective-permute-start.30 = (bf16[2,128,512]{2,1,0:T(8,128)(2,1)S(1)}, bf16[2,128,512]{2,1,0:T(8,128)(2,1)S(1)}, u32[]{:S(2)}, u32[]{:S(2)}) collective-permute-start(bf16[2,128,512]{2,1,0:T(8,128)(2,1)S(1)} %pad_maximum_fusion.5), channel_id=1, source_target_pairs={{0,134},{128,0},{2,128},{130,2},{4,130},{132,4},{6,132},{134,6},{1... | collective-permute-start | bytes 786440 | tf_op jit(solution)/shard_map/ppermute | solution.py:25
  95.5 3.8 %collective-permute-done.29 = bf16[2,128,512]{2,1,0:T(8,128)(2,1)S(1)} collective-permute-done((bf16[2,128,512]{2,1,0:T(8,128)(2,1)S(1)}, bf16[2,128,512]{2,1,0:T(8,128)(2,1)S(1)}, u32[]{:S(2)}, u32[]{:S(2)}) %collective-permute-start.29) | collective-permute-done | bytes 262176 | tf_op jit(solution)/shard_map/ppermute | solution.py:25
  99.7 3.2 %collective-permute-start.33 = (bf16[2,128,512]{2,1,0:T(8,128)(2,1)S(1)}, bf16[2,128,512]{2,1,0:T(8,128)(2,1)S(1)}, u32[]{:S(2)}, u32[]{:S(2)}) collective-permute-start(bf16[2,128,512]{2,1,0:T(8,128)(2,1)S(1)} %get-tuple-element.94), channel_id=1, source_target_pairs={{0,134},{128,0},{2,128},{130,2},{4,130},{132,4},{6,132},{134,6},{1... | collective-permute-start | bytes 786440 | tf_op jit(solution)/shard_map/ppermute | solution.py:25
  104.3 3.6 %collective-permute-done.32 = bf16[2,128,512]{2,1,0:T(8,128)(2,1)S(1)} collective-permute-done((bf16[2,128,512]{2,1,0:T(8,128)(2,1)S(1)}, bf16[2,128,512]{2,1,0:T(8,128)(2,1)S(1)}, u32[]{:S(2)}, u32[]{:S(2)}) %collective-permute-start.32) | collective-permute-done | bytes 262176 | tf_op jit(solution)/shard_map/ppermute | solution.py:25
  108.2 3.0 %collective-permute-start.36 = (bf16[2,128,512]{2,1,0:T(8,128)(2,1)S(1)}, bf16[2,128,512]{2,1,0:T(8,128)(2,1)S(1)}, u32[]{:S(2)}, u32[]{:S(2)}) collective-permute-start(bf16[2,128,512]{2,1,0:T(8,128)(2,1)S(1)} %get-tuple-element.89), channel_id=1, source_target_pairs={{0,134},{128,0},{2,128},{130,2},{4,130},{132,4},{6,132},{134,6},{1... | collective-permute-start | bytes 786440 | tf_op jit(solution)/shard_map/ppermute | solution.py:25
  111.2 3.9 %collective-permute-done.36 = bf16[2,128,512]{2,1,0:T(8,128)(2,1)S(1)} collective-permute-done((bf16[2,128,512]{2,1,0:T(8,128)(2,1)S(1)}, bf16[2,128,512]{2,1,0:T(8,128)(2,1)S(1)}, u32[]{:S(2)}, u32[]{:S(2)}) %collective-permute-start.36) | collective-permute-done | bytes 262176 | tf_op jit(solution)/shard_map/ppermute | solution.py:25
  115.1 3.7 %collective-permute-done.35 = bf16[2,128,512]{2,1,0:T(8,128)(2,1)S(1)} collective-permute-done((bf16[2,128,512]{2,1,0:T(8,128)(2,1)S(1)}, bf16[2,128,512]{2,1,0:T(8,128)(2,1)S(1)}, u32[]{:S(2)}, u32[]{:S(2)}) %collective-permute-start.35) | collective-permute-done | bytes 262176 | tf_op jit(solution)/shard_map/ppermute | solution.py:25
  (95 shorter events, 22.6 us)
Async XLA Ops:
  1.6 10.5 %collective-permute-start = (bf16[2,128,512]{2,1,0:T(8,128)(2,1)S(1)}, bf16[2,128,512]{2,1,0:T(8,128)(2,1)S(1)}, u32[]{:S(2)}, u32[]{:S(2)}) collective-permute-start(bf16[2,128,512]{2,1,0:T(8,128)(2,1)S(1)} %pad_maximum_fusion.2.refs_1_), channel_id=1, source_target_pairs={{0,128},{128,2},{2,130},{130,4},{4,132},{132,6},{6,134},{134,0},{1... | collective-permute-start | bytes 786440 | tf_op jit(solution)/shard_map/ppermute | solution.py:25
  1.9 10.2 %collective-permute-start.1 = (bf16[2,128,512]{2,1,0:T(8,128)(2,1)S(1)}, bf16[2,128,512]{2,1,0:T(8,128)(2,1)S(1)}, u32[]{:S(2)}, u32[]{:S(2)}) collective-permute-start(bf16[2,128,512]{2,1,0:T(8,128)(2,1)S(1)} %pad_maximum_fusion.2.refs_1_), channel_id=1, source_target_pairs={{0,134},{128,0},{2,128},{130,2},{4,130},{132,4},{6,132},{134,6},{1... | collective-permute-start | bytes 786440 | tf_op jit(solution)/shard_map/ppermute | solution.py:25
  12.1 9.8 %collective-permute-start.3 = (bf16[2,128,512]{2,1,0:T(8,128)(2,1)S(1)}, bf16[2,128,512]{2,1,0:T(8,128)(2,1)S(1)}, u32[]{:S(2)}, u32[]{:S(2)}) collective-permute-start(bf16[2,128,512]{2,1,0:T(8,128)(2,1)S(1)} %collective-permute-done.refs_9_.refs_13_), channel_id=1, source_target_pairs={{0,128},{128,2},{2,130},{130,4},{4,132},{132,6},{6,134},{134,0},{1... | collective-permute-start | bytes 786440 | tf_op jit(solution)/shard_map/ppermute | solution.py:25
  12.6 9.3 %collective-permute-start.4 = (bf16[2,128,512]{2,1,0:T(8,128)(2,1)S(1)}, bf16[2,128,512]{2,1,0:T(8,128)(2,1)S(1)}, u32[]{:S(2)}, u32[]{:S(2)}) collective-permute-start(bf16[2,128,512]{2,1,0:T(8,128)(2,1)S(1)} %collective-permute-done.1.refs_10_.refs_14_), channel_id=1, source_target_pairs={{0,134},{128,0},{2,128},{130,2},{4,130},{132,4},{6,132},{134,6},{1... | collective-permute-start | bytes 786440 | tf_op jit(solution)/shard_map/ppermute | solution.py:25
  15.4 6.5 %collective-permute-start.5 = (f32[128,1]{0,1:T(1,128)S(1)}, f32[128,1]{0,1:T(1,128)S(1)}, u32[]{:S(2)}, u32[]{:S(2)}) collective-permute-start(f32[128,1]{0,1:T(1,128)S(1)} %get-tuple-element.105), channel_id=1, source_target_pairs={{0,120},{8,0},{16,8},{24,16},{32,24},{40,32},{48,40},{56,48},{64,5... | collective-permute-start | bytes 1544 | tf_op jit(solution)/shard_map/ppermute | solution.py:29
  21.9 9.0 %collective-permute-start.6 = (bf16[2,128,512]{2,1,0:T(8,128)(2,1)S(1)}, bf16[2,128,512]{2,1,0:T(8,128)(2,1)S(1)}, u32[]{:S(2)}, u32[]{:S(2)}) collective-permute-start(bf16[2,128,512]{2,1,0:T(8,128)(2,1)S(1)} %collective-permute-done.3.refs_0_), channel_id=1, source_target_pairs={{0,128},{128,2},{2,130},{130,4},{4,132},{132,6},{6,134},{134,0},{1... | collective-permute-start | bytes 786440 | tf_op jit(solution)/shard_map/ppermute | solution.py:25
  22.7 8.2 %collective-permute-start.7 = (bf16[2,128,512]{2,1,0:T(8,128)(2,1)S(1)}, bf16[2,128,512]{2,1,0:T(8,128)(2,1)S(1)}, u32[]{:S(2)}, u32[]{:S(2)}) collective-permute-start(bf16[2,128,512]{2,1,0:T(8,128)(2,1)S(1)} %collective-permute-done.4.refs_2_), channel_id=1, source_target_pairs={{0,134},{128,0},{2,128},{130,2},{4,130},{132,4},{6,132},{134,6},{1... | collective-permute-start | bytes 786440 | tf_op jit(solution)/shard_map/ppermute | solution.py:25
  25.2 14.0 %collective-permute-start.10 = (bf16[2,2,128,512]{3,2,1,0:T(8,128)(2,1)S(1)}, bf16[2,2,128,512]{3,2,1,0:T(8,128)(2,1)S(1)}, u32[]{:S(2)}, u32[]{:S(2)}) collective-permute-start(bf16[2,2,128,512]{3,2,1,0:T(8,128)(2,1)S(1)} %pad_maximum_fusion), channel_id=1, source_target_pairs={{0,120},{8,0},{16,8},{24,16},{32,24},{40,32},{48,40},{56,48},{64,5... | collective-permute-start | bytes 1572872 | tf_op jit(solution)/shard_map/ppermute | solution.py:29
  41.8 17.6 %collective-permute-start.21 = (bf16[2,2,128,512]{3,2,1,0:T(8,128)(2,1)}, bf16[2,2,128,512]{3,2,1,0:T(8,128)(2,1)S(1)}, u32[]{:S(2)}, u32[]{:S(2)}) collective-permute-start(bf16[2,2,128,512]{3,2,1,0:T(8,128)(2,1)} %pad_maximum_fusion.1), channel_id=1, source_target_pairs={{0,120},{8,0},{16,8},{24,16},{32,24},{40,32},{48,40},{56,48},{64,5... | collective-permute-start | bytes 1572872 | tf_op jit(solution)/shard_map/ppermute | solution.py:29
  49.2 10.1 %collective-permute-start.22 = (bf16[2,2,128,512]{3,2,1,0:T(8,128)(2,1)S(1)}, bf16[2,2,128,512]{3,2,1,0:T(8,128)(2,1)S(1)}, u32[]{:S(2)}, u32[]{:S(2)}) collective-permute-start(bf16[2,2,128,512]{3,2,1,0:T(8,128)(2,1)S(1)} %collective-permute-done.10.refs_0_.refs_8_), channel_id=1, source_target_pairs={{0,1},{1,0},{2,3},{3,2},{4,5},{5,4},{6,7},{7,6},{8,9},{9,8},{10,11... | collective-permute-start | bytes 1572872 | tf_op jit(solution)/shard_map/ppermute | solution.py:37
  66.0 15.5 %collective-permute-start.19 = (bf16[4,2,128,512]{3,2,1,0:T(8,128)(2,1)S(1)}, bf16[4,2,128,512]{3,2,1,0:T(8,128)(2,1)S(1)}, u32[]{:S(2)}, u32[]{:S(2)}) collective-permute-start(bf16[4,2,128,512]{3,2,1,0:T(8,128)(2,1)S(1)} %get-tuple-element.64), channel_id=1, source_target_pairs={{0,1},{1,0},{2,3},{3,2},{4,5},{5,4},{6,7},{7,6},{8,9},{9,8},{10,11... | collective-permute-start | bytes 3145736 | tf_op jit(solution)/shard_map/ppermute | solution.py:37
  66.3 23.5 %collective-permute-start.20 = (bf16[4,2,128,512]{3,2,1,0:T(8,128)(2,1)S(1)}, bf16[4,2,128,512]{3,2,1,0:T(8,128)(2,1)S(1)}, u32[]{:S(2)}, u32[]{:S(2)}) collective-permute-start(bf16[4,2,128,512]{3,2,1,0:T(8,128)(2,1)S(1)} %get-tuple-element.66), channel_id=1, source_target_pairs={{0,1},{1,0},{2,3},{3,2},{4,5},{5,4},{6,7},{7,6},{8,9},{9,8},{10,11... | collective-permute-start | bytes 3145736 | tf_op jit(solution)/shard_map/ppermute | solution.py:37
  68.8 12.6 %collective-permute-start.25 = (bf16[2,128,512]{2,1,0:T(8,128)(2,1)S(1)}, bf16[2,128,512]{2,1,0:T(8,128)(2,1)S(1)}, u32[]{:S(2)}, u32[]{:S(2)}) collective-permute-start(bf16[2,128,512]{2,1,0:T(8,128)(2,1)S(1)} %get-tuple-element.93), channel_id=1, source_target_pairs={{0,8},{8,16},{16,24},{24,32},{32,40},{40,48},{48,56},{56,64},{64,7... | collective-permute-start | bytes 786440 | tf_op jit(solution)/shard_map/ppermute | solution.py:29
  77.5 12.4 %collective-permute-start.28 = (bf16[2,128,512]{2,1,0:T(8,128)(2,1)S(1)}, bf16[2,128,512]{2,1,0:T(8,128)(2,1)S(1)}, u32[]{:S(2)}, u32[]{:S(2)}) collective-permute-start(bf16[2,128,512]{2,1,0:T(8,128)(2,1)S(1)} %get-tuple-element.92), channel_id=1, source_target_pairs={{0,8},{8,16},{16,24},{24,32},{32,40},{40,48},{48,56},{56,64},{64,7... | collective-permute-start | bytes 786440 | tf_op jit(solution)/shard_map/ppermute | solution.py:29
  81.6 8.3 %collective-permute-start.26 = (bf16[128,512]{1,0:T(8,128)(2,1)S(1)}, bf16[128,512]{1,0:T(8,128)(2,1)S(1)}, u32[]{:S(2)}, u32[]{:S(2)}) collective-permute-start(bf16[128,512]{1,0:T(8,128)(2,1)S(1)} %get-tuple-element.101), channel_id=1, source_target_pairs={{0,128},{128,2},{2,130},{130,4},{4,132},{132,6},{6,134},{134,0},{1... | collective-permute-start | bytes 393224 | tf_op jit(solution)/shard_map/ppermute | solution.py:25
  81.7 8.2 %collective-permute-start.27 = (bf16[128,512]{1,0:T(8,128)(2,1)S(1)}, bf16[128,512]{1,0:T(8,128)(2,1)S(1)}, u32[]{:S(2)}, u32[]{:S(2)}) collective-permute-start(bf16[128,512]{1,0:T(8,128)(2,1)S(1)} %get-tuple-element.100), channel_id=1, source_target_pairs={{0,134},{128,0},{2,128},{130,2},{4,130},{132,4},{6,132},{134,6},{1... | collective-permute-start | bytes 393224 | tf_op jit(solution)/shard_map/ppermute | solution.py:25
  84.9 10.6 %collective-permute-start.31 = (bf16[2,128,512]{2,1,0:T(8,128)(2,1)S(1)}, bf16[2,128,512]{2,1,0:T(8,128)(2,1)S(1)}, u32[]{:S(2)}, u32[]{:S(2)}) collective-permute-start(bf16[2,128,512]{2,1,0:T(8,128)(2,1)S(1)} %get-tuple-element.91), channel_id=1, source_target_pairs={{0,8},{8,16},{16,24},{24,32},{32,40},{40,48},{48,56},{56,64},{64,7... | collective-permute-start | bytes 786440 | tf_op jit(solution)/shard_map/ppermute | solution.py:29
  90.2 9.1 %collective-permute-start.29 = (bf16[2,128,512]{2,1,0:T(8,128)(2,1)S(1)}, bf16[2,128,512]{2,1,0:T(8,128)(2,1)S(1)}, u32[]{:S(2)}, u32[]{:S(2)}) collective-permute-start(bf16[2,128,512]{2,1,0:T(8,128)(2,1)S(1)} %pad_maximum_fusion.4), channel_id=1, source_target_pairs={{0,128},{128,2},{2,130},{130,4},{4,132},{132,6},{6,134},{134,0},{1... | collective-permute-start | bytes 786440 | tf_op jit(solution)/shard_map/ppermute | solution.py:25
  90.4 8.9 %collective-permute-start.30 = (bf16[2,128,512]{2,1,0:T(8,128)(2,1)S(1)}, bf16[2,128,512]{2,1,0:T(8,128)(2,1)S(1)}, u32[]{:S(2)}, u32[]{:S(2)}) collective-permute-start(bf16[2,128,512]{2,1,0:T(8,128)(2,1)S(1)} %pad_maximum_fusion.5), channel_id=1, source_target_pairs={{0,134},{128,0},{2,128},{130,2},{4,130},{132,4},{6,132},{134,6},{1... | collective-permute-start | bytes 786440 | tf_op jit(solution)/shard_map/ppermute | solution.py:25
  93.7 10.6 %collective-permute-start.34 = (bf16[2,128,512]{2,1,0:T(8,128)(2,1)S(1)}, bf16[2,128,512]{2,1,0:T(8,128)(2,1)S(1)}, u32[]{:S(2)}, u32[]{:S(2)}) collective-permute-start(bf16[2,128,512]{2,1,0:T(8,128)(2,1)S(1)} %get-tuple-element.90), channel_id=1, source_target_pairs={{0,8},{8,16},{16,24},{24,32},{32,40},{40,48},{48,56},{56,64},{64,7... | collective-permute-start | bytes 786440 | tf_op jit(solution)/shard_map/ppermute | solution.py:29
  99.6 8.2 %collective-permute-start.32 = (bf16[2,128,512]{2,1,0:T(8,128)(2,1)S(1)}, bf16[2,128,512]{2,1,0:T(8,128)(2,1)S(1)}, u32[]{:S(2)}, u32[]{:S(2)}) collective-permute-start(bf16[2,128,512]{2,1,0:T(8,128)(2,1)S(1)} %get-tuple-element.95), channel_id=1, source_target_pairs={{0,128},{128,2},{2,130},{130,4},{4,132},{132,6},{6,134},{134,0},{1... | collective-permute-start | bytes 786440 | tf_op jit(solution)/shard_map/ppermute | solution.py:25
  99.7 8.1 %collective-permute-start.33 = (bf16[2,128,512]{2,1,0:T(8,128)(2,1)S(1)}, bf16[2,128,512]{2,1,0:T(8,128)(2,1)S(1)}, u32[]{:S(2)}, u32[]{:S(2)}) collective-permute-start(bf16[2,128,512]{2,1,0:T(8,128)(2,1)S(1)} %get-tuple-element.94), channel_id=1, source_target_pairs={{0,134},{128,0},{2,128},{130,2},{4,130},{132,4},{6,132},{134,6},{1... | collective-permute-start | bytes 786440 | tf_op jit(solution)/shard_map/ppermute | solution.py:25
  108.2 6.9 %collective-permute-start.36 = (bf16[2,128,512]{2,1,0:T(8,128)(2,1)S(1)}, bf16[2,128,512]{2,1,0:T(8,128)(2,1)S(1)}, u32[]{:S(2)}, u32[]{:S(2)}) collective-permute-start(bf16[2,128,512]{2,1,0:T(8,128)(2,1)S(1)} %get-tuple-element.89), channel_id=1, source_target_pairs={{0,134},{128,0},{2,128},{130,2},{4,130},{132,4},{6,132},{134,6},{1... | collective-permute-start | bytes 786440 | tf_op jit(solution)/shard_map/ppermute | solution.py:25
  111.2 7.6 %collective-permute-start.35 = (bf16[2,128,512]{2,1,0:T(8,128)(2,1)S(1)}, bf16[2,128,512]{2,1,0:T(8,128)(2,1)S(1)}, u32[]{:S(2)}, u32[]{:S(2)}) collective-permute-start(bf16[2,128,512]{2,1,0:T(8,128)(2,1)S(1)} %get-tuple-element.88), channel_id=1, source_target_pairs={{0,128},{128,2},{2,130},{130,4},{4,132},{132,6},{6,134},{134,0},{1... | collective-permute-start | bytes 786440 | tf_op jit(solution)/shard_map/ppermute | solution.py:25
  (17 other events, 69.5 us)
where the time goes:
time: 120 us
  starting transfers between devices  46.8 us (39%)
  waiting for transfers between devices  40.5 us (34%)
  Pallas kernels  20.7 us (17%)
  other arithmetic  5.45 us (5%)
  local copies, waits for them, and re-layouts  3.94 us (3%)
  between operations  2.29 us (2%)
    ppermute x16, starting transfers between devices, along_z(): return lax.ppermute(array, ('zlo', 'zhi'), pairs)  27.2 us
    ppermute x16, waiting for transfers between devices, along_z(): return lax.ppermute(array, ('zlo', 'zhi'), pairs)  18.2 us
    ppermute x7, starting transfers between devices, along_plane(): lax.ppermute(array, ('x', 'y'), [(i, (i + by) % 16) for i in range(16)])  17 us
    ppermute x7, waiting for transfers between devices, along_plane(): lax.ppermute(array, ('x', 'y'), [(i, (i + by) % 16) for i in range(16)])  15.4 us
    pallas_call x1, Pallas kernels, shards(): pl.pallas_call(weights_kernel, out_shape=(shape(512, 4096), shape(256, 40...  8.33 us
    pallas_call x1, Pallas kernels, shards(): pl.pallas_call(near_kernel, out_shape=(QUAD,) * 4 + (shape(3, 384, 128),)...  7.87 us
    ppermute x13, waiting for transfers between devices, other_core(): return lax.ppermute(array, 'core', [(0, 1), (1, 0)])  6.15 us
    pallas_call x1, Pallas kernels, shards(): pl.pallas_call(left_kernel, out_shape=(QUAD,) * 2 + (shape(1, 384, 128),)...  4.47 us
  transfers between devices with their start and end apart: 37, of which 21 were waited for; matrix products, arithmetic and copies ran while one was open for 5% of the time, Pallas kernels for 14%

commit v1 on v0

--- a/solution.py
+++ b/solution.py
@@ -390,10 +390,14 @@
     own_peer, far_peer = other_core(own_peer), other_core(far_peer)
     left_peer = other_core(left_peer)
 
-    def rightward(i):
-        return along_plane(narrow(wide(left_out[i]) + wide(left_peer[i])), 1)
-
-    right = {3: rightward(3)}
+    def left_sum(i):
+        return wide(left_out[i]) + wide(left_peer[i])
+
+    def rightward(sums):
+        return along_plane(narrow(sums), 1)
+
+    right = {0: rightward(left_sum(0))}
+    moved = lax.ppermute(narrow(left_sum(3)), "zhi", [(i, (i + 2) % 4) for i in range(4)])
     grad_in, grad_down = pl.pallas_call(
         weights_kernel,
         out_shape=(shape(512, 4096), shape(256, 4096)),
@@ -416,29 +420,27 @@
         compiler_params=params(16),
         name="weights",
     )(where, turn, left_turn, *own, *lefts, *far)
-    right[3], grad_in, grad_down = together(right[3], grad_in, grad_down)
-
-    def near_part(i, half=slice(None)):
-        extra = jnp.where(first, 0.0, wide(right[i][half]))
-        return wide(own_out[i][half]) + wide(own_peer[i][half]) + extra
+
+    def near_part(i):
+        part = wide(own_out[i]) + wide(own_peer[i])
+        return part + jnp.where(first, 0.0, wide(right[i])) if i in right else part
 
     def far_part(i):
-        extra = jnp.where(first, wide(right[i]), 0.0)
-        return wide(far_out[i]) + wide(far_peer[i]) + extra
+        part = wide(far_out[i]) + wide(far_peer[i])
+        return part + jnp.where(first, wide(right[i]), 0.0) if i in right else part
 
     top = narrow(near_part(3))
     up, down = along_z(top[0], 1), along_z(top[1], -1)
-    right[0] = rightward(0)
-    up, down, right[0] = together(up, down, right[0])
+    up, down, right[0], grad_in, grad_down = together(up, down, right[0], grad_in, grad_down)
     high, low = far_part(3), far_part(0)
     up = narrow(jnp.stack([high[0] + wide(up), high[1]]))
     down = narrow(jnp.stack([low[0], low[1] + wide(down)]))
     up, down = along_z(up, 1), along_z(down, -1)
-    right[2] = rightward(2)
-    up, down, right[2] = together(up, down, right[2])
+    right[2] = rightward(left_sum(2))
+    up, down, right[2], moved = together(up, down, right[2], moved)
     up, down = narrow(near_part(2) + wide(up)), narrow(near_part(0) + wide(down))
     up, down = along_z(up, 1), along_z(down, -1)
-    right[1] = rightward(1)
+    right[1] = rightward(left_sum(1) + wide(moved))
     up, down, right[1] = together(up, down, right[1])
     up, down = narrow(far_part(2) + wide(up)), narrow(far_part(1) + wide(down))
     up, down = along_z(up, 1), along_z(down, -1)

time: 120 us -> 125 us (1.042)
  the two profiles are of different devices: /device:TPU:0 before, /device:TPU:64 now
where the time goes in v1:
time: 125 us; the launch traced here: 123 us
  waiting for transfers between devices  46.1 us (37%)
  starting transfers between devices  44.4 us (36%)
  Pallas kernels  20.7 us (17%)
  other arithmetic  5.36 us (4%)
  local copies, waits for them, and re-layouts  3.94 us (3%)
  between operations  2.24 us (2%)
    ppermute x16, waiting for transfers between devices, along_z(): return lax.ppermute(array, ('zlo', 'zhi'), pairs)  20.8 us
    ppermute x16, starting transfers between devices, along_z(): return lax.ppermute(array, ('zlo', 'zhi'), pairs)  18.5 us
    ppermute x6, waiting for transfers between devices, along_plane(): lax.ppermute(array, ('x', 'y'), [(i, (i + by) % 16) for i in range(16)])  17.9 us
    ppermute x6, starting transfers between devices, along_plane(): lax.ppermute(array, ('x', 'y'), [(i, (i + by) % 16) for i in range(16)])  17.5 us
    pallas_call x1, Pallas kernels, shards(): pl.pallas_call(weights_kernel, out_shape=(shape(512, 4096), shape(256, 40...  8.33 us
    pallas_call x1, Pallas kernels, shards(): pl.pallas_call(near_kernel, out_shape=(QUAD,) * 4 + (shape(3, 384, 128),)...  7.9 us
    ppermute x13, waiting for transfers between devices, other_core(): return lax.ppermute(array, 'core', [(0, 1), (1, 0)])  4.72 us
    pallas_call x1, Pallas kernels, shards(): pl.pallas_call(left_kernel, out_shape=(QUAD,) * 2 + (shape(1, 384, 128),)...  4.47 us
  transfers between devices with their start and end apart: 37, of which 21 were waited for; matrix products, arithmetic and copies ran while one was open for 4% of the time, Pallas kernels for 17%

profile of v1, /device:TPU:64, one launch (start us, length us, event | category | flops | bytes accessed | tf_op | source)
XLA Modules:
  0.0 122.7 jit_solution(5615899497174409686)
XLA Ops:
  1.6 2.0 %collective-permute-start = (bf16[2,128,512]{2,1,0:T(8,128)(2,1)S(1)}, bf16[2,128,512]{2,1,0:T(8,128)(2,1)S(1)}, u32[]{:S(2)}, u32[]{:S(2)}) collective-permute-start(bf16[2,128,512]{2,1,0:T(8,128)(2,1)S(1)} %pad_maximum_fusion.2.refs_1_), channel_id=1, source_target_pairs={{0,128},{128,2},{2,130},{130,4},{4,132},{132,6},{6,134},{134,0},{1... | collective-permute-start | bytes 786440 | tf_op jit(solution)/shard_map/ppermute | solution.py:25
  5.5 3.1 %collective-permute-start.2 = (f32[128,2]{0,1:T(2,128)S(1)}, f32[128,2]{0,1:T(2,128)S(1)}, u32[]{:S(2)}, u32[]{:S(2)}) collective-permute-start(f32[128,2]{0,1:T(2,128)S(1)} %get-tuple-element.100), channel_id=1, source_target_pairs={{0,128},{8,136},{16,144},{24,152},{32,160},{40,168},{48,176},{56,1... | collective-permute-start | bytes 3080 | tf_op jit(solution)/shard_map/ppermute | solution.py:33
  11.3 1.5 %collective-permute-done.2 = f32[128,2]{0,1:T(2,128)S(1)} collective-permute-done((f32[128,2]{0,1:T(2,128)S(1)}, f32[128,2]{0,1:T(2,128)S(1)}, u32[]{:S(2)}, u32[]{:S(2)}) %collective-permute-start.2) | collective-permute-done | bytes 1056 | tf_op jit(solution)/shard_map/ppermute | solution.py:33
  12.8 2.9 %collective-permute-start.3 = (bf16[2,128,512]{2,1,0:T(8,128)(2,1)S(1)}, bf16[2,128,512]{2,1,0:T(8,128)(2,1)S(1)}, u32[]{:S(2)}, u32[]{:S(2)}) collective-permute-start(bf16[2,128,512]{2,1,0:T(8,128)(2,1)S(1)} %collective-permute-done.refs_9_.refs_13_), channel_id=1, source_target_pairs={{0,128},{128,2},{2,130},{130,4},{4,132},{132,6},{6,134},{134,0},{1... | collective-permute-start | bytes 786440 | tf_op jit(solution)/shard_map/ppermute | solution.py:25
  15.7 5.3 %collective-permute-start.5 = (f32[128,1]{0,1:T(1,128)S(1)}, f32[128,1]{0,1:T(1,128)S(1)}, u32[]{:S(2)}, u32[]{:S(2)}) collective-permute-start(f32[128,1]{0,1:T(1,128)S(1)} %get-tuple-element.102), channel_id=1, source_target_pairs={{0,120},{8,0},{16,8},{24,16},{32,24},{40,32},{48,40},{56,48},{64,5... | collective-permute-start | bytes 1544 | tf_op jit(solution)/shard_map/ppermute | solution.py:29
  22.3 1.9 %collective-permute-start.6 = (bf16[2,128,512]{2,1,0:T(8,128)(2,1)S(1)}, bf16[2,128,512]{2,1,0:T(8,128)(2,1)S(1)}, u32[]{:S(2)}, u32[]{:S(2)}) collective-permute-start(bf16[2,128,512]{2,1,0:T(8,128)(2,1)S(1)} %collective-permute-done.3.refs_0_), channel_id=1, source_target_pairs={{0,128},{128,2},{2,130},{130,4},{4,132},{132,6},{6,134},{134,0},{1... | collective-permute-start | bytes 786440 | tf_op jit(solution)/shard_map/ppermute | solution.py:25
  24.4 5.6 %collective-permute-start.10 = (bf16[2,2,128,512]{3,2,1,0:T(8,128)(2,1)S(1)}, bf16[2,2,128,512]{3,2,1,0:T(8,128)(2,1)S(1)}, u32[]{:S(2)}, u32[]{:S(2)}) collective-permute-start(bf16[2,2,128,512]{3,2,1,0:T(8,128)(2,1)S(1)} %pad_maximum_fusion), channel_id=1, source_target_pairs={{0,120},{8,0},{16,8},{24,16},{32,24},{40,32},{48,40},{56,48},{64,5... | collective-permute-start | bytes 1572872 | tf_op jit(solution)/shard_map/ppermute | solution.py:29
  30.7 2.8 %collective-permute-start.8 = (bf16[128,512]{1,0:T(8,128)(2,1)S(1)}, bf16[128,512]{1,0:T(8,128)(2,1)S(1)}, u32[]{:S(2)}, u32[]{:S(2)}) collective-permute-start(bf16[128,512]{1,0:T(8,128)(2,1)S(1)} %slice_bitcast_fusion.7), channel_id=1, source_target_pairs={{0,128},{128,2},{2,130},{130,4},{4,132},{132,6},{6,134},{134,0},{1... | collective-permute-start | bytes 393224 | tf_op jit(solution)/shard_map/ppermute | solution.py:25
  34.1 1.8 %collective-permute-done.8 = bf16[128,512]{1,0:T(8,128)(2,1)S(1)} collective-permute-done((bf16[128,512]{1,0:T(8,128)(2,1)S(1)}, bf16[128,512]{1,0:T(8,128)(2,1)S(1)}, u32[]{:S(2)}, u32[]{:S(2)}) %collective-permute-start.8) | collective-permute-done | bytes 131104 | tf_op jit(solution)/shard_map/ppermute | solution.py:25
  36.0 2.5 %collective-permute-done.9 = bf16[128,512]{1,0:T(8,128)(2,1)S(1)} collective-permute-done((bf16[128,512]{1,0:T(8,128)(2,1)S(1)}, bf16[128,512]{1,0:T(8,128)(2,1)S(1)}, u32[]{:S(2)}, u32[]{:S(2)}) %collective-permute-start.9) | collective-permute-done | bytes 131104 | tf_op jit(solution)/shard_map/ppermute | solution.py:25
  41.0 5.7 %collective-permute-start.23 = (bf16[2,2,128,512]{3,2,1,0:T(8,128)(2,1)}, bf16[2,2,128,512]{3,2,1,0:T(8,128)(2,1)S(1)}, u32[]{:S(2)}, u32[]{:S(2)}) collective-permute-start(bf16[2,2,128,512]{3,2,1,0:T(8,128)(2,1)} %pad_maximum_fusion.1), channel_id=1, source_target_pairs={{0,120},{8,0},{16,8},{24,16},{32,24},{40,32},{48,40},{56,48},{64,5... | collective-permute-start | bytes 1572872 | tf_op jit(solution)/shard_map/ppermute | solution.py:29
  49.5 7.9 %near.1 = (bf16[4,2,128,512]{3,2,1,0:T(8,128)(2,1)S(1)}, bf16[4,2,128,512]{3,2,1,0:T(8,128)(2,1)S(1)}, bf16[4,2,128,512]{3,2,1,0:T(8,128)(2,1)S(1)}, bf16[4,2,12...) custom-call(s32[5]{0:T(128)S(1)} %stack.82.where, f32[128,4]{1,0:T(8,128)S(1)} %copy.17.weights, ...), custom_call_target="tpu_custom_call" | custom-call | tf_op jit(solution)/shard_map/near/pallas_call | solution.py:354
  60.4 4.5 %left.1 = (bf16[4,2,128,512]{3,2,1,0:T(8,128)(2,1)S(1)}, bf16[4,2,128,512]{3,2,1,0:T(8,128)(2,1)S(1)}, bf16[1,384,128]{2,1,0:T(8,128)(2,1)S(1)}) custom-call(s32[5]{0:T(128)S(1)} %stack.82.where, f32[128,4]{1,0:T(8,128)S(1)} %copy.17.weights, bf16[512,4096]{1,0:T(8,128)(2,1)} %bitcast.80, bf16[256,4096]{1,0:T(8,128)(2,1)} %bitcast.82, ...), custom_call_target="tpu_custom_call" | custom-call | tf_op jit(solution)/shard_map/left/pallas_call | solution.py:374
  65.6 1.8 %collective-permute-start.21 = (bf16[128,512]{1,0:T(8,128)(2,1)S(1)}, bf16[128,512]{1,0:T(8,128)(2,1)S(1)}, u32[]{:S(2)}, u32[]{:S(2)}) collective-permute-start(bf16[128,512]{1,0:T(8,128)(2,1)S(1)} %get-tuple-element.98), channel_id=1, source_target_pairs={{0,128},{128,2},{2,130},{130,4},{4,132},{132,6},{6,134},{134,0},{1... | collective-permute-start | bytes 393224 | tf_op jit(solution)/shard_map/ppermute | solution.py:25
  69.2 8.3 %weights.1 = (bf16[512,4096]{1,0:T(8,128)(2,1)}, bf16[256,4096]{1,0:T(8,128)(2,1)}) custom-call(s32[5]{0:T(128)S(1)} %stack.82.where, bf16[3,384,128]{2,1,0:T(8,128)(2,1)S(1)} %get-tuple-element.72.turn, bf16[1,384,128]{2,1,0:T(8,128)(2,1)S(1)} %get-tuple-element.73.left_turn, bf16[2,128,512]{2,1,0:T(8,128)(2,1)S(1)} %collective-permute-done.3.refs_0_, ...), custom_call_target="tpu_custom_call" | custom-call | tf_op jit(solution)/shard_map/weights/pallas_call | solution.py:401
  77.7 2.3 %collective-permute-start.31 = (bf16[2,128,512]{2,1,0:T(8,128)(2,1)S(1)}, bf16[2,128,512]{2,1,0:T(8,128)(2,1)S(1)}, u32[]{:S(2)}, u32[]{:S(2)}) collective-permute-start(bf16[2,128,512]{2,1,0:T(8,128)(2,1)S(1)} %get-tuple-element.92), channel_id=1, source_target_pairs={{0,4},{2,6},{4,0},{6,2},{1,5},{3,7},{5,1},{7,3},{8,12},{10,14},{12... | collective-permute-start | bytes 786440 | tf_op jit(solution)/shard_map/ppermute | solution.py:400
  80.5 1.5 %collective-permute-start.29 = (bf16[2,128,512]{2,1,0:T(8,128)(2,1)S(1)}, bf16[2,128,512]{2,1,0:T(8,128)(2,1)S(1)}, u32[]{:S(2)}, u32[]{:S(2)}) collective-permute-start(bf16[2,128,512]{2,1,0:T(8,128)(2,1)S(1)} %pad_maximum_fusion.5), channel_id=1, source_target_pairs={{0,134},{128,0},{2,128},{130,2},{4,130},{132,4},{6,132},{134,6},{1... | collective-permute-start | bytes 786440 | tf_op jit(solution)/shard_map/ppermute | solution.py:25
  82.9 7.1 %collective-permute-done.30 = bf16[2,128,512]{2,1,0:T(8,128)(2,1)S(1)} collective-permute-done((bf16[2,128,512]{2,1,0:T(8,128)(2,1)S(1)}, bf16[2,128,512]{2,1,0:T(8,128)(2,1)S(1)}, u32[]{:S(2)}, u32[]{:S(2)}) %collective-permute-start.30) | collective-permute-done | bytes 262176 | tf_op jit(solution)/shard_map/ppermute | solution.py:29
  91.1 8.2 %collective-permute-done.29 = bf16[2,128,512]{2,1,0:T(8,128)(2,1)S(1)} collective-permute-done((bf16[2,128,512]{2,1,0:T(8,128)(2,1)S(1)}, bf16[2,128,512]{2,1,0:T(8,128)(2,1)S(1)}, u32[]{:S(2)}, u32[]{:S(2)}) %collective-permute-start.29) | collective-permute-done | bytes 262176 | tf_op jit(solution)/shard_map/ppermute | solution.py:25
  99.3 1.9 %collective-permute-done.28 = bf16[2,128,512]{2,1,0:T(8,128)(2,1)S(1)} collective-permute-done((bf16[2,128,512]{2,1,0:T(8,128)(2,1)S(1)}, bf16[2,128,512]{2,1,0:T(8,128)(2,1)S(1)}, u32[]{:S(2)}, u32[]{:S(2)}) %collective-permute-start.28) | collective-permute-done | bytes 262176 | tf_op jit(solution)/shard_map/ppermute | solution.py:25
  102.5 2.0 %collective-permute-start.33 = (bf16[2,128,512]{2,1,0:T(8,128)(2,1)S(1)}, bf16[2,128,512]{2,1,0:T(8,128)(2,1)S(1)}, u32[]{:S(2)}, u32[]{:S(2)}) collective-permute-start(bf16[2,128,512]{2,1,0:T(8,128)(2,1)S(1)} %get-tuple-element.90), channel_id=1, source_target_pairs={{0,134},{128,0},{2,128},{130,2},{4,130},{132,4},{6,132},{134,6},{1... | collective-permute-start | bytes 786440 | tf_op jit(solution)/shard_map/ppermute | solution.py:25
  104.5 9.1 %collective-permute-done.34 = bf16[2,128,512]{2,1,0:T(8,128)(2,1)S(1)} collective-permute-done((bf16[2,128,512]{2,1,0:T(8,128)(2,1)S(1)}, bf16[2,128,512]{2,1,0:T(8,128)(2,1)S(1)}, u32[]{:S(2)}, u32[]{:S(2)}) %collective-permute-start.34) | collective-permute-done | bytes 262176 | tf_op jit(solution)/shard_map/ppermute | solution.py:29
  114.0 2.0 %collective-permute-start.36 = (bf16[2,128,512]{2,1,0:T(8,128)(2,1)S(1)}, bf16[2,128,512]{2,1,0:T(8,128)(2,1)S(1)}, u32[]{:S(2)}, u32[]{:S(2)}) collective-permute-start(bf16[2,128,512]{2,1,0:T(8,128)(2,1)S(1)} %get-tuple-element.89), channel_id=1, source_target_pairs={{0,134},{128,0},{2,128},{130,2},{4,130},{132,4},{6,132},{134,6},{1... | collective-permute-start | bytes 786440 | tf_op jit(solution)/shard_map/ppermute | solution.py:25
  116.0 5.7 %collective-permute-done.35 = bf16[2,128,512]{2,1,0:T(8,128)(2,1)S(1)} collective-permute-done((bf16[2,128,512]{2,1,0:T(8,128)(2,1)S(1)}, bf16[2,128,512]{2,1,0:T(8,128)(2,1)S(1)}, u32[]{:S(2)}, u32[]{:S(2)}) %collective-permute-start.35) | collective-permute-done | bytes 262176 | tf_op jit(solution)/shard_map/ppermute | solution.py:25
  (97 shorter events, 22.9 us)
Async XLA Ops:
  1.6 11.2 %collective-permute-start = (bf16[2,128,512]{2,1,0:T(8,128)(2,1)S(1)}, bf16[2,128,512]{2,1,0:T(8,128)(2,1)S(1)}, u32[]{:S(2)}, u32[]{:S(2)}) collective-permute-start(bf16[2,128,512]{2,1,0:T(8,128)(2,1)S(1)} %pad_maximum_fusion.2.refs_1_), channel_id=1, source_target_pairs={{0,128},{128,2},{2,130},{130,4},{4,132},{132,6},{6,134},{134,0},{1... | collective-permute-start | bytes 786440 | tf_op jit(solution)/shard_map/ppermute | solution.py:25
  3.6 9.2 %collective-permute-start.1 = (bf16[2,128,512]{2,1,0:T(8,128)(2,1)S(1)}, bf16[2,128,512]{2,1,0:T(8,128)(2,1)S(1)}, u32[]{:S(2)}, u32[]{:S(2)}) collective-permute-start(bf16[2,128,512]{2,1,0:T(8,128)(2,1)S(1)} %pad_maximum_fusion.2.refs_1_), channel_id=1, source_target_pairs={{0,134},{128,0},{2,128},{130,2},{4,130},{132,4},{6,132},{134,6},{1... | collective-permute-start | bytes 786440 | tf_op jit(solution)/shard_map/ppermute | solution.py:25
  5.5 7.4 %collective-permute-start.2 = (f32[128,2]{0,1:T(2,128)S(1)}, f32[128,2]{0,1:T(2,128)S(1)}, u32[]{:S(2)}, u32[]{:S(2)}) collective-permute-start(f32[128,2]{0,1:T(2,128)S(1)} %get-tuple-element.100), channel_id=1, source_target_pairs={{0,128},{8,136},{16,144},{24,152},{32,160},{40,168},{48,176},{56,1... | collective-permute-start | bytes 3080 | tf_op jit(solution)/shard_map/ppermute | solution.py:33
  12.8 9.5 %collective-permute-start.3 = (bf16[2,128,512]{2,1,0:T(8,128)(2,1)S(1)}, bf16[2,128,512]{2,1,0:T(8,128)(2,1)S(1)}, u32[]{:S(2)}, u32[]{:S(2)}) collective-permute-start(bf16[2,128,512]{2,1,0:T(8,128)(2,1)S(1)} %collective-permute-done.refs_9_.refs_13_), channel_id=1, source_target_pairs={{0,128},{128,2},{2,130},{130,4},{4,132},{132,6},{6,134},{134,0},{1... | collective-permute-start | bytes 786440 | tf_op jit(solution)/shard_map/ppermute | solution.py:25
  15.7 6.6 %collective-permute-start.4 = (bf16[2,128,512]{2,1,0:T(8,128)(2,1)S(1)}, bf16[2,128,512]{2,1,0:T(8,128)(2,1)S(1)}, u32[]{:S(2)}, u32[]{:S(2)}) collective-permute-start(bf16[2,128,512]{2,1,0:T(8,128)(2,1)S(1)} %collective-permute-done.1.refs_10_.refs_14_), channel_id=1, source_target_pairs={{0,134},{128,0},{2,128},{130,2},{4,130},{132,4},{6,132},{134,6},{1... | collective-permute-start | bytes 786440 | tf_op jit(solution)/shard_map/ppermute | solution.py:25
  15.7 6.6 %collective-permute-start.5 = (f32[128,1]{0,1:T(1,128)S(1)}, f32[128,1]{0,1:T(1,128)S(1)}, u32[]{:S(2)}, u32[]{:S(2)}) collective-permute-start(f32[128,1]{0,1:T(1,128)S(1)} %get-tuple-element.102), channel_id=1, source_target_pairs={{0,120},{8,0},{16,8},{24,16},{32,24},{40,32},{48,40},{56,48},{64,5... | collective-permute-start | bytes 1544 | tf_op jit(solution)/shard_map/ppermute | solution.py:29
  22.3 7.8 %collective-permute-start.6 = (bf16[2,128,512]{2,1,0:T(8,128)(2,1)S(1)}, bf16[2,128,512]{2,1,0:T(8,128)(2,1)S(1)}, u32[]{:S(2)}, u32[]{:S(2)}) collective-permute-start(bf16[2,128,512]{2,1,0:T(8,128)(2,1)S(1)} %collective-permute-done.3.refs_0_), channel_id=1, source_target_pairs={{0,128},{128,2},{2,130},{130,4},{4,132},{132,6},{6,134},{134,0},{1... | collective-permute-start | bytes 786440 | tf_op jit(solution)/shard_map/ppermute | solution.py:25
  24.3 6.4 %collective-permute-start.7 = (bf16[2,128,512]{2,1,0:T(8,128)(2,1)S(1)}, bf16[2,128,512]{2,1,0:T(8,128)(2,1)S(1)}, u32[]{:S(2)}, u32[]{:S(2)}) collective-permute-start(bf16[2,128,512]{2,1,0:T(8,128)(2,1)S(1)} %collective-permute-done.4.refs_2_), channel_id=1, source_target_pairs={{0,134},{128,0},{2,128},{130,2},{4,130},{132,4},{6,132},{134,6},{1... | collective-permute-start | bytes 786440 | tf_op jit(solution)/shard_map/ppermute | solution.py:25
  24.4 14.1 %collective-permute-start.10 = (bf16[2,2,128,512]{3,2,1,0:T(8,128)(2,1)S(1)}, bf16[2,2,128,512]{3,2,1,0:T(8,128)(2,1)S(1)}, u32[]{:S(2)}, u32[]{:S(2)}) collective-permute-start(bf16[2,2,128,512]{3,2,1,0:T(8,128)(2,1)S(1)} %pad_maximum_fusion), channel_id=1, source_target_pairs={{0,120},{8,0},{16,8},{24,16},{32,24},{40,32},{48,40},{56,48},{64,5... | collective-permute-start | bytes 1572872 | tf_op jit(solution)/shard_map/ppermute | solution.py:29
  41.0 17.5 %collective-permute-start.23 = (bf16[2,2,128,512]{3,2,1,0:T(8,128)(2,1)}, bf16[2,2,128,512]{3,2,1,0:T(8,128)(2,1)S(1)}, u32[]{:S(2)}, u32[]{:S(2)}) collective-permute-start(bf16[2,2,128,512]{3,2,1,0:T(8,128)(2,1)} %pad_maximum_fusion.1), channel_id=1, source_target_pairs={{0,120},{8,0},{16,8},{24,16},{32,24},{40,32},{48,40},{56,48},{64,5... | collective-permute-start | bytes 1572872 | tf_op jit(solution)/shard_map/ppermute | solution.py:29
  48.4 10.6 %collective-permute-start.24 = (bf16[2,2,128,512]{3,2,1,0:T(8,128)(2,1)S(1)}, bf16[2,2,128,512]{3,2,1,0:T(8,128)(2,1)S(1)}, u32[]{:S(2)}, u32[]{:S(2)}) collective-permute-start(bf16[2,2,128,512]{3,2,1,0:T(8,128)(2,1)S(1)} %collective-permute-done.10.refs_0_.refs_8_), channel_id=1, source_target_pairs={{0,1},{1,0},{2,3},{3,2},{4,5},{5,4},{6,7},{7,6},{8,9},{9,8},{10,11... | collective-permute-start | bytes 1572872 | tf_op jit(solution)/shard_map/ppermute | solution.py:37
  58.5 7.0 %collective-permute-start.19 = (bf16[4,2,128,512]{3,2,1,0:T(8,128)(2,1)S(1)}, bf16[4,2,128,512]{3,2,1,0:T(8,128)(2,1)S(1)}, u32[]{:S(2)}, u32[]{:S(2)}) collective-permute-start(bf16[4,2,128,512]{3,2,1,0:T(8,128)(2,1)S(1)} %get-tuple-element.64), channel_id=1, source_target_pairs={{0,1},{1,0},{2,3},{3,2},{4,5},{5,4},{6,7},{7,6},{8,9},{9,8},{10,11... | collective-permute-start | bytes 3145736 | tf_op jit(solution)/shard_map/ppermute | solution.py:37
  65.6 14.4 %collective-permute-start.21 = (bf16[128,512]{1,0:T(8,128)(2,1)S(1)}, bf16[128,512]{1,0:T(8,128)(2,1)S(1)}, u32[]{:S(2)}, u32[]{:S(2)}) collective-permute-start(bf16[128,512]{1,0:T(8,128)(2,1)S(1)} %get-tuple-element.98), channel_id=1, source_target_pairs={{0,128},{128,2},{2,130},{130,4},{4,132},{132,6},{6,134},{134,0},{1... | collective-permute-start | bytes 393224 | tf_op jit(solution)/shard_map/ppermute | solution.py:25
  67.4 12.6 %collective-permute-start.22 = (bf16[128,512]{1,0:T(8,128)(2,1)S(1)}, bf16[128,512]{1,0:T(8,128)(2,1)S(1)}, u32[]{:S(2)}, u32[]{:S(2)}) collective-permute-start(bf16[128,512]{1,0:T(8,128)(2,1)S(1)} %get-tuple-element.97), channel_id=1, source_target_pairs={{0,134},{128,0},{2,128},{130,2},{4,130},{132,4},{6,132},{134,6},{1... | collective-permute-start | bytes 393224 | tf_op jit(solution)/shard_map/ppermute | solution.py:25
  67.9 12.3 %collective-permute-start.27 = (bf16[2,128,512]{2,1,0:T(8,128)(2,1)S(1)}, bf16[2,128,512]{2,1,0:T(8,128)(2,1)S(1)}, u32[]{:S(2)}, u32[]{:S(2)}) collective-permute-start(bf16[2,128,512]{2,1,0:T(8,128)(2,1)S(1)} %get-tuple-element.94), channel_id=1, source_target_pairs={{0,8},{8,16},{16,24},{24,32},{32,40},{40,48},{48,56},{56,64},{64,7... | collective-permute-start | bytes 786440 | tf_op jit(solution)/shard_map/ppermute | solution.py:29
  77.6 12.4 %collective-permute-start.30 = (bf16[2,128,512]{2,1,0:T(8,128)(2,1)S(1)}, bf16[2,128,512]{2,1,0:T(8,128)(2,1)S(1)}, u32[]{:S(2)}, u32[]{:S(2)}) collective-permute-start(bf16[2,128,512]{2,1,0:T(8,128)(2,1)S(1)} %get-tuple-element.93), channel_id=1, source_target_pairs={{0,8},{8,16},{16,24},{24,32},{32,40},{40,48},{48,56},{56,64},{64,7... | collective-permute-start | bytes 786440 | tf_op jit(solution)/shard_map/ppermute | solution.py:29
  77.7 13.5 %collective-permute-start.31 = (bf16[2,128,512]{2,1,0:T(8,128)(2,1)S(1)}, bf16[2,128,512]{2,1,0:T(8,128)(2,1)S(1)}, u32[]{:S(2)}, u32[]{:S(2)}) collective-permute-start(bf16[2,128,512]{2,1,0:T(8,128)(2,1)S(1)} %get-tuple-element.92), channel_id=1, source_target_pairs={{0,4},{2,6},{4,0},{6,2},{1,5},{3,7},{5,1},{7,3},{8,12},{10,14},{12... | collective-permute-start | bytes 786440 | tf_op jit(solution)/shard_map/ppermute | solution.py:400
  80.5 18.8 %collective-permute-start.29 = (bf16[2,128,512]{2,1,0:T(8,128)(2,1)S(1)}, bf16[2,128,512]{2,1,0:T(8,128)(2,1)S(1)}, u32[]{:S(2)}, u32[]{:S(2)}) collective-permute-start(bf16[2,128,512]{2,1,0:T(8,128)(2,1)S(1)} %pad_maximum_fusion.5), channel_id=1, source_target_pairs={{0,134},{128,0},{2,128},{130,2},{4,130},{132,4},{6,132},{134,6},{1... | collective-permute-start | bytes 786440 | tf_op jit(solution)/shard_map/ppermute | solution.py:25
  82.1 19.1 %collective-permute-start.28 = (bf16[2,128,512]{2,1,0:T(8,128)(2,1)S(1)}, bf16[2,128,512]{2,1,0:T(8,128)(2,1)S(1)}, u32[]{:S(2)}, u32[]{:S(2)}) collective-permute-start(bf16[2,128,512]{2,1,0:T(8,128)(2,1)S(1)} %pad_maximum_fusion.4), channel_id=1, source_target_pairs={{0,128},{128,2},{2,130},{130,4},{4,132},{132,6},{6,134},{134,0},{1... | collective-permute-start | bytes 786440 | tf_op jit(solution)/shard_map/ppermute | solution.py:25
  101.4 12.3 %collective-permute-start.34 = (bf16[2,128,512]{2,1,0:T(8,128)(2,1)S(1)}, bf16[2,128,512]{2,1,0:T(8,128)(2,1)S(1)}, u32[]{:S(2)}, u32[]{:S(2)}) collective-permute-start(bf16[2,128,512]{2,1,0:T(8,128)(2,1)S(1)} %fusion.17), channel_id=1, source_target_pairs={{0,8},{8,16},{16,24},{24,32},{32,40},{40,48},{48,56},{56,64},{64,7... | collective-permute-start | bytes 786440 | tf_op jit(solution)/shard_map/ppermute | solution.py:29
  102.4 11.2 %collective-permute-start.32 = (bf16[2,128,512]{2,1,0:T(8,128)(2,1)S(1)}, bf16[2,128,512]{2,1,0:T(8,128)(2,1)S(1)}, u32[]{:S(2)}, u32[]{:S(2)}) collective-permute-start(bf16[2,128,512]{2,1,0:T(8,128)(2,1)S(1)} %get-tuple-element.91), channel_id=1, source_target_pairs={{0,128},{128,2},{2,130},{130,4},{4,132},{132,6},{6,134},{134,0},{1... | collective-permute-start | bytes 786440 | tf_op jit(solution)/shard_map/ppermute | solution.py:25
  102.5 11.2 %collective-permute-start.33 = (bf16[2,128,512]{2,1,0:T(8,128)(2,1)S(1)}, bf16[2,128,512]{2,1,0:T(8,128)(2,1)S(1)}, u32[]{:S(2)}, u32[]{:S(2)}) collective-permute-start(bf16[2,128,512]{2,1,0:T(8,128)(2,1)S(1)} %get-tuple-element.90), channel_id=1, source_target_pairs={{0,134},{128,0},{2,128},{130,2},{4,130},{132,4},{6,132},{134,6},{1... | collective-permute-start | bytes 786440 | tf_op jit(solution)/shard_map/ppermute | solution.py:25
  113.9 7.8 %collective-permute-start.35 = (bf16[2,128,512]{2,1,0:T(8,128)(2,1)S(1)}, bf16[2,128,512]{2,1,0:T(8,128)(2,1)S(1)}, u32[]{:S(2)}, u32[]{:S(2)}) collective-permute-start(bf16[2,128,512]{2,1,0:T(8,128)(2,1)S(1)} %get-tuple-element.88), channel_id=1, source_target_pairs={{0,128},{128,2},{2,130},{130,4},{4,132},{132,6},{6,134},{134,0},{1... | collective-permute-start | bytes 786440 | tf_op jit(solution)/shard_map/ppermute | solution.py:25
  114.0 7.8 %collective-permute-start.36 = (bf16[2,128,512]{2,1,0:T(8,128)(2,1)S(1)}, bf16[2,128,512]{2,1,0:T(8,128)(2,1)S(1)}, u32[]{:S(2)}, u32[]{:S(2)}) collective-permute-start(bf16[2,128,512]{2,1,0:T(8,128)(2,1)S(1)} %get-tuple-element.89), channel_id=1, source_target_pairs={{0,134},{128,0},{2,128},{130,2},{4,130},{132,4},{6,132},{134,6},{1... | collective-permute-start | bytes 786440 | tf_op jit(solution)/shard_map/ppermute | solution.py:25
  (17 other events, 67.9 us)

commit v2 on v1

--- a/solution.py
+++ b/solution.py
@@ -431,13 +431,15 @@
 
     top = narrow(near_part(3))
     up, down = along_z(top[0], 1), along_z(top[1], -1)
-    up, down, right[0], grad_in, grad_down = together(up, down, right[0], grad_in, grad_down)
+    up, down, right[0], moved, grad_in, grad_down = together(
+        up, down, right[0], moved, grad_in, grad_down
+    )
     high, low = far_part(3), far_part(0)
     up = narrow(jnp.stack([high[0] + wide(up), high[1]]))
     down = narrow(jnp.stack([low[0], low[1] + wide(down)]))
     up, down = along_z(up, 1), along_z(down, -1)
     right[2] = rightward(left_sum(2))
-    up, down, right[2], moved = together(up, down, right[2], moved)
+    up, down, right[2] = together(up, down, right[2])
     up, down = narrow(near_part(2) + wide(up)), narrow(near_part(0) + wide(down))
     up, down = along_z(up, 1), along_z(down, -1)
     right[1] = rightward(left_sum(1) + wide(moved))

time: 125 us -> 117 us (0.936)
  waiting for transfers between devices: 46.1 us -> 33.2 us
  starting transfers between devices: 44.4 us -> 50.2 us
    ppermute x6, waiting for transfers between devices: 17.9 us -> 6.06 us  [along_plane(): lax.ppermute(array, ('x', 'y'), [(i, (i + by) % 16) for i in range(16)])]
    ppermute x16, starting transfers between devices: 18.5 us -> 25 us  [along_z(): return lax.ppermute(array, ('zlo', 'zhi'), pairs)]
  transfers between devices with their start and end apart: 37 -> 37, of which waited for: 21 -> 22; matrix products, arithmetic and copies ran while one was open for 4% -> 5% of each run, Pallas kernels for 17% -> 18%
where the time goes in v2:
time: 117 us; the launch traced here: 116 us
  starting transfers between devices  50.2 us (43%)
  waiting for transfers between devices  33.2 us (28%)
  Pallas kernels  20.7 us (18%)
  other arithmetic  5.37 us (5%)
  local copies, waits for them, and re-layouts  3.94 us (3%)
  between operations  2.25 us (2%)
    ppermute x16, starting transfers between devices, along_z(): return lax.ppermute(array, ('zlo', 'zhi'), pairs)  25 us
    ppermute x16, waiting for transfers between devices, along_z(): return lax.ppermute(array, ('zlo', 'zhi'), pairs)  21.8 us
    ppermute x6, starting transfers between devices, along_plane(): lax.ppermute(array, ('x', 'y'), [(i, (i + by) % 16) for i in range(16)])  16.8 us
    pallas_call x1, Pallas kernels, shards(): pl.pallas_call(weights_kernel, out_shape=(shape(512, 4096), shape(256, 40...  8.33 us
    pallas_call x1, Pallas kernels, shards(): pl.pallas_call(near_kernel, out_shape=(QUAD,) * 4 + (shape(3, 384, 128),)...  7.9 us
    ppermute x6, waiting for transfers between devices, along_plane(): lax.ppermute(array, ('x', 'y'), [(i, (i + by) % 16) for i in range(16)])  6.06 us
    pallas_call x1, Pallas kernels, shards(): pl.pallas_call(left_kernel, out_shape=(QUAD,) * 2 + (shape(1, 384, 128),)...  4.47 us
    ppermute x13, waiting for transfers between devices, other_core(): return lax.ppermute(array, 'core', [(0, 1), (1, 0)])  3.63 us
  transfers between devices with their start and end apart: 37, of which 22 were waited for; matrix products, arithmetic and copies ran while one was open for 5% of the time, Pallas kernels for 18%

profile of v2, /device:TPU:64, one launch (start us, length us, event | category | flops | bytes accessed | tf_op | source)
XLA Modules:
  0.0 115.6 jit_solution(351868413525614056)
XLA Ops:
  1.6 2.0 %collective-permute-start = (bf16[2,128,512]{2,1,0:T(8,128)(2,1)S(1)}, bf16[2,128,512]{2,1,0:T(8,128)(2,1)S(1)}, u32[]{:S(2)}, u32[]{:S(2)}) collective-permute-start(bf16[2,128,512]{2,1,0:T(8,128)(2,1)S(1)} %pad_maximum_fusion.2.refs_1_), channel_id=1, source_target_pairs={{0,128},{128,2},{2,130},{130,4},{4,132},{132,6},{6,134},{134,0},{1... | collective-permute-start | bytes 786440 | tf_op jit(solution)/shard_map/ppermute | solution.py:25
  5.5 3.1 %collective-permute-start.2 = (f32[128,2]{0,1:T(2,128)S(1)}, f32[128,2]{0,1:T(2,128)S(1)}, u32[]{:S(2)}, u32[]{:S(2)}) collective-permute-start(f32[128,2]{0,1:T(2,128)S(1)} %get-tuple-element.100), channel_id=1, source_target_pairs={{0,128},{8,136},{16,144},{24,152},{32,160},{40,168},{48,176},{56,1... | collective-permute-start | bytes 3080 | tf_op jit(solution)/shard_map/ppermute | solution.py:33
  12.8 2.9 %collective-permute-start.3 = (bf16[2,128,512]{2,1,0:T(8,128)(2,1)S(1)}, bf16[2,128,512]{2,1,0:T(8,128)(2,1)S(1)}, u32[]{:S(2)}, u32[]{:S(2)}) collective-permute-start(bf16[2,128,512]{2,1,0:T(8,128)(2,1)S(1)} %collective-permute-done.refs_9_.refs_13_), channel_id=1, source_target_pairs={{0,128},{128,2},{2,130},{130,4},{4,132},{132,6},{6,134},{134,0},{1... | collective-permute-start | bytes 786440 | tf_op jit(solution)/shard_map/ppermute | solution.py:25
  15.7 5.3 %collective-permute-start.5 = (f32[128,1]{0,1:T(1,128)S(1)}, f32[128,1]{0,1:T(1,128)S(1)}, u32[]{:S(2)}, u32[]{:S(2)}) collective-permute-start(f32[128,1]{0,1:T(1,128)S(1)} %get-tuple-element.102), channel_id=1, source_target_pairs={{0,120},{8,0},{16,8},{24,16},{32,24},{40,32},{48,40},{56,48},{64,5... | collective-permute-start | bytes 1544 | tf_op jit(solution)/shard_map/ppermute | solution.py:29
  22.3 1.9 %collective-permute-start.6 = (bf16[2,128,512]{2,1,0:T(8,128)(2,1)S(1)}, bf16[2,128,512]{2,1,0:T(8,128)(2,1)S(1)}, u32[]{:S(2)}, u32[]{:S(2)}) collective-permute-start(bf16[2,128,512]{2,1,0:T(8,128)(2,1)S(1)} %collective-permute-done.3.refs_0_), channel_id=1, source_target_pairs={{0,128},{128,2},{2,130},{130,4},{4,132},{132,6},{6,134},{134,0},{1... | collective-permute-start | bytes 786440 | tf_op jit(solution)/shard_map/ppermute | solution.py:25
  24.4 5.6 %collective-permute-start.10 = (bf16[2,2,128,512]{3,2,1,0:T(8,128)(2,1)S(1)}, bf16[2,2,128,512]{3,2,1,0:T(8,128)(2,1)S(1)}, u32[]{:S(2)}, u32[]{:S(2)}) collective-permute-start(bf16[2,2,128,512]{3,2,1,0:T(8,128)(2,1)S(1)} %pad_maximum_fusion), channel_id=1, source_target_pairs={{0,120},{8,0},{16,8},{24,16},{32,24},{40,32},{48,40},{56,48},{64,5... | collective-permute-start | bytes 1572872 | tf_op jit(solution)/shard_map/ppermute | solution.py:29
  30.7 2.8 %collective-permute-start.8 = (bf16[128,512]{1,0:T(8,128)(2,1)S(1)}, bf16[128,512]{1,0:T(8,128)(2,1)S(1)}, u32[]{:S(2)}, u32[]{:S(2)}) collective-permute-start(bf16[128,512]{1,0:T(8,128)(2,1)S(1)} %slice_bitcast_fusion.7), channel_id=1, source_target_pairs={{0,128},{128,2},{2,130},{130,4},{4,132},{132,6},{6,134},{134,0},{1... | collective-permute-start | bytes 393224 | tf_op jit(solution)/shard_map/ppermute | solution.py:25
  34.1 1.8 %collective-permute-done.8 = bf16[128,512]{1,0:T(8,128)(2,1)S(1)} collective-permute-done((bf16[128,512]{1,0:T(8,128)(2,1)S(1)}, bf16[128,512]{1,0:T(8,128)(2,1)S(1)}, u32[]{:S(2)}, u32[]{:S(2)}) %collective-permute-start.8) | collective-permute-done | bytes 131104 | tf_op jit(solution)/shard_map/ppermute | solution.py:25
  36.0 2.5 %collective-permute-done.9 = bf16[128,512]{1,0:T(8,128)(2,1)S(1)} collective-permute-done((bf16[128,512]{1,0:T(8,128)(2,1)S(1)}, bf16[128,512]{1,0:T(8,128)(2,1)S(1)}, u32[]{:S(2)}, u32[]{:S(2)}) %collective-permute-start.9) | collective-permute-done | bytes 131104 | tf_op jit(solution)/shard_map/ppermute | solution.py:25
  41.0 5.7 %collective-permute-start.23 = (bf16[2,2,128,512]{3,2,1,0:T(8,128)(2,1)}, bf16[2,2,128,512]{3,2,1,0:T(8,128)(2,1)S(1)}, u32[]{:S(2)}, u32[]{:S(2)}) collective-permute-start(bf16[2,2,128,512]{3,2,1,0:T(8,128)(2,1)} %pad_maximum_fusion.1), channel_id=1, source_target_pairs={{0,120},{8,0},{16,8},{24,16},{32,24},{40,32},{48,40},{56,48},{64,5... | collective-permute-start | bytes 1572872 | tf_op jit(solution)/shard_map/ppermute | solution.py:29
  49.5 7.9 %near.1 = (bf16[4,2,128,512]{3,2,1,0:T(8,128)(2,1)S(1)}, bf16[4,2,128,512]{3,2,1,0:T(8,128)(2,1)S(1)}, bf16[4,2,128,512]{3,2,1,0:T(8,128)(2,1)S(1)}, bf16[4,2,12...) custom-call(s32[5]{0:T(128)S(1)} %stack.82.where, f32[128,4]{1,0:T(8,128)S(1)} %copy.17.weights, ...), custom_call_target="tpu_custom_call" | custom-call | tf_op jit(solution)/shard_map/near/pallas_call | solution.py:354
  60.4 4.5 %left.1 = (bf16[4,2,128,512]{3,2,1,0:T(8,128)(2,1)S(1)}, bf16[4,2,128,512]{3,2,1,0:T(8,128)(2,1)S(1)}, bf16[1,384,128]{2,1,0:T(8,128)(2,1)S(1)}) custom-call(s32[5]{0:T(128)S(1)} %stack.82.where, f32[128,4]{1,0:T(8,128)S(1)} %copy.17.weights, bf16[512,4096]{1,0:T(8,128)(2,1)} %bitcast.80, bf16[256,4096]{1,0:T(8,128)(2,1)} %bitcast.82, ...), custom_call_target="tpu_custom_call" | custom-call | tf_op jit(solution)/shard_map/left/pallas_call | solution.py:374
  65.6 1.8 %collective-permute-start.21 = (bf16[128,512]{1,0:T(8,128)(2,1)S(1)}, bf16[128,512]{1,0:T(8,128)(2,1)S(1)}, u32[]{:S(2)}, u32[]{:S(2)}) collective-permute-start(bf16[128,512]{1,0:T(8,128)(2,1)S(1)} %get-tuple-element.98), channel_id=1, source_target_pairs={{0,128},{128,2},{2,130},{130,4},{4,132},{132,6},{6,134},{134,0},{1... | collective-permute-start | bytes 393224 | tf_op jit(solution)/shard_map/ppermute | solution.py:25
  68.0 2.3 %collective-permute-start.28 = (bf16[2,128,512]{2,1,0:T(8,128)(2,1)S(1)}, bf16[2,128,512]{2,1,0:T(8,128)(2,1)S(1)}, u32[]{:S(2)}, u32[]{:S(2)}) collective-permute-start(bf16[2,128,512]{2,1,0:T(8,128)(2,1)S(1)} %get-tuple-element.93), channel_id=1, source_target_pairs={{0,4},{2,6},{4,0},{6,2},{1,5},{3,7},{5,1},{7,3},{8,12},{10,14},{12... | collective-permute-start | bytes 786440 | tf_op jit(solution)/shard_map/ppermute | solution.py:400
  70.5 8.3 %weights.1 = (bf16[512,4096]{1,0:T(8,128)(2,1)}, bf16[256,4096]{1,0:T(8,128)(2,1)}) custom-call(s32[5]{0:T(128)S(1)} %stack.82.where, bf16[3,384,128]{2,1,0:T(8,128)(2,1)S(1)} %get-tuple-element.72.turn, bf16[1,384,128]{2,1,0:T(8,128)(2,1)S(1)} %get-tuple-element.73.left_turn, bf16[2,128,512]{2,1,0:T(8,128)(2,1)S(1)} %collective-permute-done.3.refs_0_, ...), custom_call_target="tpu_custom_call" | custom-call | tf_op jit(solution)/shard_map/weights/pallas_call | solution.py:401
  80.6 6.6 %collective-permute-start.30 = (bf16[2,128,512]{2,1,0:T(8,128)(2,1)S(1)}, bf16[2,128,512]{2,1,0:T(8,128)(2,1)S(1)}, u32[]{:S(2)}, u32[]{:S(2)}) collective-permute-start(bf16[2,128,512]{2,1,0:T(8,128)(2,1)S(1)} %pad_maximum_fusion.5), channel_id=1, source_target_pairs={{0,134},{128,0},{2,128},{130,2},{4,130},{132,4},{6,132},{134,6},{1... | collective-permute-start | bytes 786440 | tf_op jit(solution)/shard_map/ppermute | solution.py:25
  88.4 2.4 %collective-permute-done.31 = bf16[2,128,512]{2,1,0:T(8,128)(2,1)S(1)} collective-permute-done((bf16[2,128,512]{2,1,0:T(8,128)(2,1)S(1)}, bf16[2,128,512]{2,1,0:T(8,128)(2,1)S(1)}, u32[]{:S(2)}, u32[]{:S(2)}) %collective-permute-start.31) | collective-permute-done | bytes 262176 | tf_op jit(solution)/shard_map/ppermute | solution.py:29
  90.9 2.2 %collective-permute-done.30 = bf16[2,128,512]{2,1,0:T(8,128)(2,1)S(1)} collective-permute-done((bf16[2,128,512]{2,1,0:T(8,128)(2,1)S(1)}, bf16[2,128,512]{2,1,0:T(8,128)(2,1)S(1)}, u32[]{:S(2)}, u32[]{:S(2)}) %collective-permute-start.30) | collective-permute-done | bytes 262176 | tf_op jit(solution)/shard_map/ppermute | solution.py:25
  93.0 2.5 %collective-permute-done.29 = bf16[2,128,512]{2,1,0:T(8,128)(2,1)S(1)} collective-permute-done((bf16[2,128,512]{2,1,0:T(8,128)(2,1)S(1)}, bf16[2,128,512]{2,1,0:T(8,128)(2,1)S(1)}, u32[]{:S(2)}, u32[]{:S(2)}) %collective-permute-start.29) | collective-permute-done | bytes 262176 | tf_op jit(solution)/shard_map/ppermute | solution.py:25
  98.8 4.3 %collective-permute-done.32 = bf16[2,128,512]{2,1,0:T(8,128)(2,1)S(1)} collective-permute-done((bf16[2,128,512]{2,1,0:T(8,128)(2,1)S(1)}, bf16[2,128,512]{2,1,0:T(8,128)(2,1)S(1)}, u32[]{:S(2)}, u32[]{:S(2)}) %collective-permute-start.32) | collective-permute-done | bytes 262176 | tf_op jit(solution)/shard_map/ppermute | solution.py:25
  103.1 1.6 %collective-permute-done.33 = bf16[2,128,512]{2,1,0:T(8,128)(2,1)S(1)} collective-permute-done((bf16[2,128,512]{2,1,0:T(8,128)(2,1)S(1)}, bf16[2,128,512]{2,1,0:T(8,128)(2,1)S(1)}, u32[]{:S(2)}, u32[]{:S(2)}) %collective-permute-start.33) | collective-permute-done | bytes 262176 | tf_op jit(solution)/shard_map/ppermute | solution.py:25
  105.0 3.3 %collective-permute-start.35 = (bf16[2,128,512]{2,1,0:T(8,128)(2,1)S(1)}, bf16[2,128,512]{2,1,0:T(8,128)(2,1)S(1)}, u32[]{:S(2)}, u32[]{:S(2)}) collective-permute-start(bf16[2,128,512]{2,1,0:T(8,128)(2,1)S(1)} %get-tuple-element.88), channel_id=1, source_target_pairs={{0,128},{128,2},{2,130},{130,4},{4,132},{132,6},{6,134},{134,0},{1... | collective-permute-start | bytes 786440 | tf_op jit(solution)/shard_map/ppermute | solution.py:25
  108.3 3.9 %collective-permute-done.35 = bf16[2,128,512]{2,1,0:T(8,128)(2,1)S(1)} collective-permute-done((bf16[2,128,512]{2,1,0:T(8,128)(2,1)S(1)}, bf16[2,128,512]{2,1,0:T(8,128)(2,1)S(1)}, u32[]{:S(2)}, u32[]{:S(2)}) %collective-permute-start.35) | collective-permute-done | bytes 262176 | tf_op jit(solution)/shard_map/ppermute | solution.py:25
  112.2 2.5 %collective-permute-done.36 = bf16[2,128,512]{2,1,0:T(8,128)(2,1)S(1)} collective-permute-done((bf16[2,128,512]{2,1,0:T(8,128)(2,1)S(1)}, bf16[2,128,512]{2,1,0:T(8,128)(2,1)S(1)}, u32[]{:S(2)}, u32[]{:S(2)}) %collective-permute-start.36) | collective-permute-done | bytes 262176 | tf_op jit(solution)/shard_map/ppermute | solution.py:25
  (97 shorter events, 25.6 us)
Async XLA Ops:
  1.6 11.2 %collective-permute-start = (bf16[2,128,512]{2,1,0:T(8,128)(2,1)S(1)}, bf16[2,128,512]{2,1,0:T(8,128)(2,1)S(1)}, u32[]{:S(2)}, u32[]{:S(2)}) collective-permute-start(bf16[2,128,512]{2,1,0:T(8,128)(2,1)S(1)} %pad_maximum_fusion.2.refs_1_), channel_id=1, source_target_pairs={{0,128},{128,2},{2,130},{130,4},{4,132},{132,6},{6,134},{134,0},{1... | collective-permute-start | bytes 786440 | tf_op jit(solution)/shard_map/ppermute | solution.py:25
  3.6 9.2 %collective-permute-start.1 = (bf16[2,128,512]{2,1,0:T(8,128)(2,1)S(1)}, bf16[2,128,512]{2,1,0:T(8,128)(2,1)S(1)}, u32[]{:S(2)}, u32[]{:S(2)}) collective-permute-start(bf16[2,128,512]{2,1,0:T(8,128)(2,1)S(1)} %pad_maximum_fusion.2.refs_1_), channel_id=1, source_target_pairs={{0,134},{128,0},{2,128},{130,2},{4,130},{132,4},{6,132},{134,6},{1... | collective-permute-start | bytes 786440 | tf_op jit(solution)/shard_map/ppermute | solution.py:25
  5.5 7.4 %collective-permute-start.2 = (f32[128,2]{0,1:T(2,128)S(1)}, f32[128,2]{0,1:T(2,128)S(1)}, u32[]{:S(2)}, u32[]{:S(2)}) collective-permute-start(f32[128,2]{0,1:T(2,128)S(1)} %get-tuple-element.100), channel_id=1, source_target_pairs={{0,128},{8,136},{16,144},{24,152},{32,160},{40,168},{48,176},{56,1... | collective-permute-start | bytes 3080 | tf_op jit(solution)/shard_map/ppermute | solution.py:33
  12.8 9.5 %collective-permute-start.3 = (bf16[2,128,512]{2,1,0:T(8,128)(2,1)S(1)}, bf16[2,128,512]{2,1,0:T(8,128)(2,1)S(1)}, u32[]{:S(2)}, u32[]{:S(2)}) collective-permute-start(bf16[2,128,512]{2,1,0:T(8,128)(2,1)S(1)} %collective-permute-done.refs_9_.refs_13_), channel_id=1, source_target_pairs={{0,128},{128,2},{2,130},{130,4},{4,132},{132,6},{6,134},{134,0},{1... | collective-permute-start | bytes 786440 | tf_op jit(solution)/shard_map/ppermute | solution.py:25
  15.7 6.6 %collective-permute-start.4 = (bf16[2,128,512]{2,1,0:T(8,128)(2,1)S(1)}, bf16[2,128,512]{2,1,0:T(8,128)(2,1)S(1)}, u32[]{:S(2)}, u32[]{:S(2)}) collective-permute-start(bf16[2,128,512]{2,1,0:T(8,128)(2,1)S(1)} %collective-permute-done.1.refs_10_.refs_14_), channel_id=1, source_target_pairs={{0,134},{128,0},{2,128},{130,2},{4,130},{132,4},{6,132},{134,6},{1... | collective-permute-start | bytes 786440 | tf_op jit(solution)/shard_map/ppermute | solution.py:25
  15.7 6.6 %collective-permute-start.5 = (f32[128,1]{0,1:T(1,128)S(1)}, f32[128,1]{0,1:T(1,128)S(1)}, u32[]{:S(2)}, u32[]{:S(2)}) collective-permute-start(f32[128,1]{0,1:T(1,128)S(1)} %get-tuple-element.102), channel_id=1, source_target_pairs={{0,120},{8,0},{16,8},{24,16},{32,24},{40,32},{48,40},{56,48},{64,5... | collective-permute-start | bytes 1544 | tf_op jit(solution)/shard_map/ppermute | solution.py:29
  22.3 7.8 %collective-permute-start.6 = (bf16[2,128,512]{2,1,0:T(8,128)(2,1)S(1)}, bf16[2,128,512]{2,1,0:T(8,128)(2,1)S(1)}, u32[]{:S(2)}, u32[]{:S(2)}) collective-permute-start(bf16[2,128,512]{2,1,0:T(8,128)(2,1)S(1)} %collective-permute-done.3.refs_0_), channel_id=1, source_target_pairs={{0,128},{128,2},{2,130},{130,4},{4,132},{132,6},{6,134},{134,0},{1... | collective-permute-start | bytes 786440 | tf_op jit(solution)/shard_map/ppermute | solution.py:25
  24.3 6.4 %collective-permute-start.7 = (bf16[2,128,512]{2,1,0:T(8,128)(2,1)S(1)}, bf16[2,128,512]{2,1,0:T(8,128)(2,1)S(1)}, u32[]{:S(2)}, u32[]{:S(2)}) collective-permute-start(bf16[2,128,512]{2,1,0:T(8,128)(2,1)S(1)} %collective-permute-done.4.refs_2_), channel_id=1, source_target_pairs={{0,134},{128,0},{2,128},{130,2},{4,130},{132,4},{6,132},{134,6},{1... | collective-permute-start | bytes 786440 | tf_op jit(solution)/shard_map/ppermute | solution.py:25
  24.4 14.1 %collective-permute-start.10 = (bf16[2,2,128,512]{3,2,1,0:T(8,128)(2,1)S(1)}, bf16[2,2,128,512]{3,2,1,0:T(8,128)(2,1)S(1)}, u32[]{:S(2)}, u32[]{:S(2)}) collective-permute-start(bf16[2,2,128,512]{3,2,1,0:T(8,128)(2,1)S(1)} %pad_maximum_fusion), channel_id=1, source_target_pairs={{0,120},{8,0},{16,8},{24,16},{32,24},{40,32},{48,40},{56,48},{64,5... | collective-permute-start | bytes 1572872 | tf_op jit(solution)/shard_map/ppermute | solution.py:29
  41.0 17.5 %collective-permute-start.23 = (bf16[2,2,128,512]{3,2,1,0:T(8,128)(2,1)}, bf16[2,2,128,512]{3,2,1,0:T(8,128)(2,1)S(1)}, u32[]{:S(2)}, u32[]{:S(2)}) collective-permute-start(bf16[2,2,128,512]{3,2,1,0:T(8,128)(2,1)} %pad_maximum_fusion.1), channel_id=1, source_target_pairs={{0,120},{8,0},{16,8},{24,16},{32,24},{40,32},{48,40},{56,48},{64,5... | collective-permute-start | bytes 1572872 | tf_op jit(solution)/shard_map/ppermute | solution.py:29
  48.4 10.6 %collective-permute-start.24 = (bf16[2,2,128,512]{3,2,1,0:T(8,128)(2,1)S(1)}, bf16[2,2,128,512]{3,2,1,0:T(8,128)(2,1)S(1)}, u32[]{:S(2)}, u32[]{:S(2)}) collective-permute-start(bf16[2,2,128,512]{3,2,1,0:T(8,128)(2,1)S(1)} %collective-permute-done.10.refs_0_.refs_8_), channel_id=1, source_target_pairs={{0,1},{1,0},{2,3},{3,2},{4,5},{5,4},{6,7},{7,6},{8,9},{9,8},{10,11... | collective-permute-start | bytes 1572872 | tf_op jit(solution)/shard_map/ppermute | solution.py:37
  58.5 7.0 %collective-permute-start.19 = (bf16[4,2,128,512]{3,2,1,0:T(8,128)(2,1)S(1)}, bf16[4,2,128,512]{3,2,1,0:T(8,128)(2,1)S(1)}, u32[]{:S(2)}, u32[]{:S(2)}) collective-permute-start(bf16[4,2,128,512]{3,2,1,0:T(8,128)(2,1)S(1)} %get-tuple-element.64), channel_id=1, source_target_pairs={{0,1},{1,0},{2,3},{3,2},{4,5},{5,4},{6,7},{7,6},{8,9},{9,8},{10,11... | collective-permute-start | bytes 3145736 | tf_op jit(solution)/shard_map/ppermute | solution.py:37
  65.6 13.3 %collective-permute-start.21 = (bf16[128,512]{1,0:T(8,128)(2,1)S(1)}, bf16[128,512]{1,0:T(8,128)(2,1)S(1)}, u32[]{:S(2)}, u32[]{:S(2)}) collective-permute-start(bf16[128,512]{1,0:T(8,128)(2,1)S(1)} %get-tuple-element.98), channel_id=1, source_target_pairs={{0,128},{128,2},{2,130},{130,4},{4,132},{132,6},{6,134},{134,0},{1... | collective-permute-start | bytes 393224 | tf_op jit(solution)/shard_map/ppermute | solution.py:25
  67.4 11.5 %collective-permute-start.22 = (bf16[128,512]{1,0:T(8,128)(2,1)S(1)}, bf16[128,512]{1,0:T(8,128)(2,1)S(1)}, u32[]{:S(2)}, u32[]{:S(2)}) collective-permute-start(bf16[128,512]{1,0:T(8,128)(2,1)S(1)} %get-tuple-element.97), channel_id=1, source_target_pairs={{0,134},{128,0},{2,128},{130,2},{4,130},{132,4},{6,132},{134,6},{1... | collective-permute-start | bytes 393224 | tf_op jit(solution)/shard_map/ppermute | solution.py:25
  67.9 12.3 %collective-permute-start.27 = (bf16[2,128,512]{2,1,0:T(8,128)(2,1)S(1)}, bf16[2,128,512]{2,1,0:T(8,128)(2,1)S(1)}, u32[]{:S(2)}, u32[]{:S(2)}) collective-permute-start(bf16[2,128,512]{2,1,0:T(8,128)(2,1)S(1)} %get-tuple-element.94), channel_id=1, source_target_pairs={{0,8},{8,16},{16,24},{24,32},{32,40},{40,48},{48,56},{56,64},{64,7... | collective-permute-start | bytes 786440 | tf_op jit(solution)/shard_map/ppermute | solution.py:29
  68.0 12.4 %collective-permute-start.28 = (bf16[2,128,512]{2,1,0:T(8,128)(2,1)S(1)}, bf16[2,128,512]{2,1,0:T(8,128)(2,1)S(1)}, u32[]{:S(2)}, u32[]{:S(2)}) collective-permute-start(bf16[2,128,512]{2,1,0:T(8,128)(2,1)S(1)} %get-tuple-element.93), channel_id=1, source_target_pairs={{0,4},{2,6},{4,0},{6,2},{1,5},{3,7},{5,1},{7,3},{8,12},{10,14},{12... | collective-permute-start | bytes 786440 | tf_op jit(solution)/shard_map/ppermute | solution.py:400
  78.8 12.1 %collective-permute-start.31 = (bf16[2,128,512]{2,1,0:T(8,128)(2,1)S(1)}, bf16[2,128,512]{2,1,0:T(8,128)(2,1)S(1)}, u32[]{:S(2)}, u32[]{:S(2)}) collective-permute-start(bf16[2,128,512]{2,1,0:T(8,128)(2,1)S(1)} %get-tuple-element.92), channel_id=1, source_target_pairs={{0,8},{8,16},{16,24},{24,32},{32,40},{40,48},{48,56},{56,64},{64,7... | collective-permute-start | bytes 786440 | tf_op jit(solution)/shard_map/ppermute | solution.py:29
  80.6 12.4 %collective-permute-start.30 = (bf16[2,128,512]{2,1,0:T(8,128)(2,1)S(1)}, bf16[2,128,512]{2,1,0:T(8,128)(2,1)S(1)}, u32[]{:S(2)}, u32[]{:S(2)}) collective-permute-start(bf16[2,128,512]{2,1,0:T(8,128)(2,1)S(1)} %pad_maximum_fusion.5), channel_id=1, source_target_pairs={{0,134},{128,0},{2,128},{130,2},{4,130},{132,4},{6,132},{134,6},{1... | collective-permute-start | bytes 786440 | tf_op jit(solution)/shard_map/ppermute | solution.py:25
  87.3 8.2 %collective-permute-start.29 = (bf16[2,128,512]{2,1,0:T(8,128)(2,1)S(1)}, bf16[2,128,512]{2,1,0:T(8,128)(2,1)S(1)}, u32[]{:S(2)}, u32[]{:S(2)}) collective-permute-start(bf16[2,128,512]{2,1,0:T(8,128)(2,1)S(1)} %pad_maximum_fusion.4), channel_id=1, source_target_pairs={{0,128},{128,2},{2,130},{130,4},{4,132},{132,6},{6,134},{134,0},{1... | collective-permute-start | bytes 786440 | tf_op jit(solution)/shard_map/ppermute | solution.py:25
  88.4 10.4 %collective-permute-start.34 = (bf16[2,128,512]{2,1,0:T(8,128)(2,1)S(1)}, bf16[2,128,512]{2,1,0:T(8,128)(2,1)S(1)}, u32[]{:S(2)}, u32[]{:S(2)}) collective-permute-start(bf16[2,128,512]{2,1,0:T(8,128)(2,1)S(1)} %fusion.17), channel_id=1, source_target_pairs={{0,8},{8,16},{16,24},{24,32},{32,40},{40,48},{48,56},{56,64},{64,7... | collective-permute-start | bytes 786440 | tf_op jit(solution)/shard_map/ppermute | solution.py:29
  95.8 7.3 %collective-permute-start.32 = (bf16[2,128,512]{2,1,0:T(8,128)(2,1)S(1)}, bf16[2,128,512]{2,1,0:T(8,128)(2,1)S(1)}, u32[]{:S(2)}, u32[]{:S(2)}) collective-permute-start(bf16[2,128,512]{2,1,0:T(8,128)(2,1)S(1)} %get-tuple-element.91), channel_id=1, source_target_pairs={{0,128},{128,2},{2,130},{130,4},{4,132},{132,6},{6,134},{134,0},{1... | collective-permute-start | bytes 786440 | tf_op jit(solution)/shard_map/ppermute | solution.py:25
  97.2 7.5 %collective-permute-start.33 = (bf16[2,128,512]{2,1,0:T(8,128)(2,1)S(1)}, bf16[2,128,512]{2,1,0:T(8,128)(2,1)S(1)}, u32[]{:S(2)}, u32[]{:S(2)}) collective-permute-start(bf16[2,128,512]{2,1,0:T(8,128)(2,1)S(1)} %get-tuple-element.90), channel_id=1, source_target_pairs={{0,134},{128,0},{2,128},{130,2},{4,130},{132,4},{6,132},{134,6},{1... | collective-permute-start | bytes 786440 | tf_op jit(solution)/shard_map/ppermute | solution.py:25
  105.0 7.2 %collective-permute-start.35 = (bf16[2,128,512]{2,1,0:T(8,128)(2,1)S(1)}, bf16[2,128,512]{2,1,0:T(8,128)(2,1)S(1)}, u32[]{:S(2)}, u32[]{:S(2)}) collective-permute-start(bf16[2,128,512]{2,1,0:T(8,128)(2,1)S(1)} %get-tuple-element.88), channel_id=1, source_target_pairs={{0,128},{128,2},{2,130},{130,4},{4,132},{132,6},{6,134},{134,0},{1... | collective-permute-start | bytes 786440 | tf_op jit(solution)/shard_map/ppermute | solution.py:25
  108.3 6.4 %collective-permute-start.36 = (bf16[2,128,512]{2,1,0:T(8,128)(2,1)S(1)}, bf16[2,128,512]{2,1,0:T(8,128)(2,1)S(1)}, u32[]{:S(2)}, u32[]{:S(2)}) collective-permute-start(bf16[2,128,512]{2,1,0:T(8,128)(2,1)S(1)} %get-tuple-element.89), channel_id=1, source_target_pairs={{0,134},{128,0},{2,128},{130,2},{4,130},{132,4},{6,132},{134,6},{1... | collective-permute-start | bytes 786440 | tf_op jit(solution)/shard_map/ppermute | solution.py:25
  (17 other events, 69.2 us)
